TPU v7x, 512 devices: a whole 4x8x8 slice. The times are simulated.
512 devices in a mesh: net: 128 (over z, y, core), scen: 4 (over x).
Axes of the slice: x: 4, y: 8, z: 8, core: 2. Of those that a mesh axis runs over, the one named last changes fastest.
Arguments:
- volt_mag: float32 [30720, 128], P('net', 'scen'), parts along dimension 1, may hold values from 0.94 to 1.06
- volt_ang: float32 [30720, 128], P('net', 'scen'), parts along dimension 1, may hold values from -0.5 to 0.5
- gradient: float32 [30720, 2, 128], P('net', None, 'scen'), parts along dimension 2, may hold values from -40 to 40
- branch_from: int32 [40960], P('net'), may hold values from 0 to 239, as said below
- branch_to: int32 [40960], P('net'), may hold values from 0 to 479, as said below
- branch_count: int32 [128], P('net'), may hold values from 160 to 320, as said below
- boundary: int32 [30720], P('net'), may hold values from 0 to 239, as said below
- conductance: float32 [40960], P('net'), may hold values from 0.2 to 2
- susceptance: float32 [40960], P('net'), may hold values from 1 to 10
- duals: float32 [2, 40960, 128], P(None, 'net', 'scen'), parts along dimension 2, may hold values from 0.02 to 0.2
- slacks: float32 [2, 40960, 128], P(None, 'net', 'scen'), parts along dimension 2, may hold values from 0.2 to 2
- gen_bus: int32 [5120], P('net'), may hold values from 0 to 239
- gen_curvature: float32 [5120], P('net'), may hold values from 1 to 10
Outputs:
- search_step: float32 [30720, 2, 128], P('net', None, 'scen'), parts along dimension 2
- residual: float32 [30720, 2, 128], P('net', None, 'scen'), parts along dimension 2
There are 4 independent parts, one for each index of `scen`. A program takes and returns all parts, laid end to end along the dimension named above; an argument that names none is the same for every part. Nothing has to cross between parts.
Inputs may be any that keep to these rules, and one draw needn't show every extreme that they name: `branch_from`: A bus index within the branch's own device. A branch whose branch_to is 240 + e with e >= 0 starts at boundary entry e of its own device. `branch_to`: below 240: a bus of the same device other than the from-bus. 240 + e for e < 120: entry e of the previous device's list toward this device; 360 + e: entry e of the next device's list toward this device. Only the first 240 slots of a device end at a neighbour, each such value at most once a device; the first device has no ends of the first kind, the last none of the second. `branch_count`: slots at or past a device's count contribute nothing. Some device is full in every draw. `boundary`: per device 2 * 120 distinct local buses: the first 120 face the previous device, the rest the next device.
All inputs are finite; a program needn't handle non-finite values.
Results may differ from a plain program's by a relative error of at most 0.0003.
Values sent between devices are 32-bit elements; how exact they have to be, the bound alone decides.
A program may use at most 64 MiB of HBM per device.

v0:
```python
import jax
import jax.numpy as jnp
from jax import lax
from jax.sharding import PartitionSpec as P

ITERS = 4


barrier_weight = 0.01
volt_low = 0.9
volt_high = 1.1
angle_reg = 0.5


def shifted(array, axis, by):
    peers = lax.axis_size(axis)
    pairs = [(i, i + by) for i in range(peers) if 0 <= i + by < peers]
    return lax.ppermute(array, axis, pairs)


def branch_blocks(
    magnitude_from,
    angle_from,
    magnitude_to,
    angle_to,
    conduct,
    suscept,
    weight_active,
    weight_reactive,
):
    angle_diff = angle_from - angle_to
    cosine_diff = jnp.cos(angle_diff)
    sine_diff = jnp.sin(angle_diff)
    flow_along = conduct * cosine_diff + suscept * sine_diff
    flow_across = conduct * sine_diff - suscept * cosine_diff
    cross_term = magnitude_from * magnitude_to
    active_rows = (
        2.0 * conduct * magnitude_from - magnitude_to * flow_along,
        cross_term * flow_across,
        -magnitude_from * flow_along,
        -cross_term * flow_across,
    )
    reactive_rows = (
        -2.0 * suscept * magnitude_from - magnitude_to * flow_across,
        -cross_term * flow_along,
        -magnitude_from * flow_across,
        cross_term * flow_along,
    )

    def block_entry(left_index, right_index):
        return (
            weight_active * active_rows[left_index] * active_rows[right_index]
            + weight_reactive * reactive_rows[left_index] * reactive_rows[right_index]
        )

    from_block = jnp.stack([block_entry(0, 0), block_entry(0, 1), block_entry(1, 1)], axis=1)
    to_block = jnp.stack([block_entry(2, 2), block_entry(2, 3), block_entry(3, 3)], axis=1)
    cross_block = jnp.stack(
        [block_entry(0, 2), block_entry(0, 3), block_entry(1, 2), block_entry(1, 3)], axis=1
    )
    return (from_block, to_block, cross_block)


def apply_cross(matrix_block, vector):
    return jnp.stack(
        [
            matrix_block[:, 0] * vector[:, 0] + matrix_block[:, 1] * vector[:, 1],
            matrix_block[:, 2] * vector[:, 0] + matrix_block[:, 3] * vector[:, 1],
        ],
        axis=1,
    )


def apply_cross_transposed(matrix_block, vector):
    return jnp.stack(
        [
            matrix_block[:, 0] * vector[:, 0] + matrix_block[:, 2] * vector[:, 1],
            matrix_block[:, 1] * vector[:, 0] + matrix_block[:, 3] * vector[:, 1],
        ],
        axis=1,
    )


def scenario_sum(left_vec, right_vec):
    return jnp.sum(left_vec * right_vec, axis=(0, 1))


def widen(values):
    return values[None, None, :]


def body(
    volt_mag,
    volt_ang,
    gradient,
    branch_from,
    branch_to,
    branch_count,
    boundary,
    conductance,
    susceptance,
    duals,
    slacks,
    gen_bus,
    gen_curvature,
):
    bus_count = volt_mag.shape[0]
    ghost_count = boundary.shape[0] // 2
    extended_size = bus_count + 2 * ghost_count
    slot_count = branch_from.shape[0]
    left_list = boundary[:ghost_count]
    right_list = boundary[ghost_count:]
    left_ghost = slice(bus_count, bus_count + ghost_count)
    right_ghost = slice(bus_count + ghost_count, extended_size)
    return_plan = (
        (-1, left_ghost, right_list, right_ghost),
        (1, right_ghost, left_list, left_ghost),
    )

    def share_vector(values):
        pieces = [values]
        for direction in (1, -1):
            outgoing = jnp.take(values, right_list if direction == 1 else left_list, axis=0)
            pieces.append(shifted(outgoing, "net", direction))
        return jnp.concatenate(pieces, axis=0)

    bus_state = jnp.stack([volt_mag, volt_ang], axis=1)
    pieces = [bus_state]
    for share_direction in (1, -1):
        outgoing = jnp.take(bus_state, right_list if share_direction == 1 else left_list, axis=0)
        pieces.append(shifted(outgoing, "net", share_direction))
    extended_state = jnp.concatenate(pieces, axis=0)
    from_state = jnp.take(extended_state, branch_from, axis=0)
    to_state = jnp.take(extended_state, branch_to, axis=0)
    live_mask = (jnp.arange(slot_count) < branch_count[0]).astype(jnp.float32)[:, None]
    weight_active = live_mask * duals[0] / slacks[0]
    weight_reactive = live_mask * duals[1] / slacks[1]
    from_block, to_block, cross_block = branch_blocks(
        from_state[:, 0],
        from_state[:, 1],
        to_state[:, 0],
        to_state[:, 1],
        conductance[:, None],
        susceptance[:, None],
        weight_active,
        weight_reactive,
    )
    diag_extended = jax.ops.segment_sum(
        from_block, branch_from, num_segments=extended_size
    ) + jax.ops.segment_sum(to_block, branch_to, num_segments=extended_size)
    diag_local = diag_extended[:bus_count]
    for direction, ghost_rows, target_rows, source_rows in return_plan:
        arrived_diag = shifted(diag_extended[ghost_rows], "net", direction)
        diag_local = diag_local.at[target_rows].add(arrived_diag)
    gen_table = (gen_bus[None, :] == jnp.arange(bus_count)[:, None]).astype(jnp.float32)
    gen_sum = jnp.dot(gen_table, gen_curvature, precision=lax.Precision.HIGHEST)[:, None]
    barrier = barrier_weight / jnp.square(volt_mag - volt_low) + barrier_weight / jnp.square(
        volt_high - volt_mag
    )
    diag_vv = diag_local[:, 0] + barrier + gen_sum
    diag_va = diag_local[:, 1]
    diag_aa = diag_local[:, 2] + angle_reg + gen_sum
    determinant = diag_vv * diag_aa - diag_va * diag_va
    inverse_vv = diag_aa / determinant
    inverse_va = -diag_va / determinant
    inverse_aa = diag_vv / determinant

    def precondition(vector):
        return jnp.stack(
            [
                inverse_vv * vector[:, 0] + inverse_va * vector[:, 1],
                inverse_va * vector[:, 0] + inverse_aa * vector[:, 1],
            ],
            axis=1,
        )

    update_field = jnp.zeros_like(gradient)
    residual = gradient

    def energy_of(residual_now, scaled_now):
        return lax.psum(scenario_sum(residual_now, scaled_now), "net")

    scaled = precondition(residual)
    search = scaled
    energy = energy_of(residual, scaled)
    for iteration in range(ITERS):
        extended = share_vector(search)
        from_values = jnp.take(extended, branch_from, axis=0)
        to_values = jnp.take(extended, branch_to, axis=0)
        from_terms = apply_cross(cross_block, to_values)
        to_terms = apply_cross_transposed(cross_block, from_values)
        result = jnp.stack(
            [
                diag_vv * search[:, 0] + diag_va * search[:, 1],
                diag_va * search[:, 0] + diag_aa * search[:, 1],
            ],
            axis=1,
        )
        summed = jax.ops.segment_sum(
            from_terms, branch_from, num_segments=extended_size
        ) + jax.ops.segment_sum(to_terms, branch_to, num_segments=extended_size)
        local_sum = result + summed[:bus_count]
        for apply_direction, apply_ghost_rows, apply_target_rows, apply_source_rows in return_plan:
            arrived = shifted(summed[apply_ghost_rows], "net", apply_direction)
            local_sum = local_sum.at[apply_target_rows].add(arrived)
        step_size = energy / lax.psum(scenario_sum(search, local_sum), "net")
        update_field = update_field + widen(step_size) * search
        residual = residual - widen(step_size) * local_sum
        if iteration + 1 < ITERS:
            scaled = precondition(residual)
            energy_next = energy_of(residual, scaled)
            search = scaled + widen(energy_next / energy) * search
            energy = energy_next
    return (update_field, residual)


def solution(mesh):
    placed = (
        P("net", "scen"),
        P("net", "scen"),
        P("net", None, "scen"),
        P("net"),
        P("net"),
        P("net"),
        P("net"),
        P("net"),
        P("net"),
        P(None, "net", "scen"),
        P(None, "net", "scen"),
        P("net"),
        P("net"),
    )
    return jax.shard_map(
        body,
        mesh=mesh,
        in_specs=placed,
        out_specs=(P("net", None, "scen"), P("net", None, "scen")),
        check_vma=False,
    )
```

profile of v0, /device:TPU:258, one launch (start us, length us, event | category | flops | bytes accessed | tf_op | source)
XLA Modules:
  0.0 2067.8 jit_solution(2405154826822002641)
XLA Ops:
  6.3 7.0 collective-permute-start.1
  18.1 2.0 gather_fusion.3
  22.2 11.9 scatter_fusion.1
  34.3 11.9 scatter_fusion
  46.6 7.1 collective-permute-start.2
  57.4 5.0 scatter_fusion.2
  62.4 2.2 collective-permute-done.3
  64.6 5.0 scatter_fusion.3
  74.6 7.0 collective-permute-start.5
  83.5 2.0 gather_fusion.7
  88.5 11.9 scatter_fusion.5
  100.6 11.9 scatter_fusion.4
  112.9 7.0 collective-permute-start.6
  119.9 2.1 collective-permute-start.7
  122.3 5.0 scatter_fusion.6
  127.3 2.1 collective-permute-done.7
  129.4 5.0 scatter_fusion.7
  134.7 249.9 %all-reduce = (f32[32]{0:T(128)S(1)}, f32[32]{0:T(128)S(1)}) all-reduce(f32[32]{0:T(128)S(1)} %get-tuple-element.11, f32[32]{0:T(128)S(1)} %get-tuple-element.10), channel_id=1, replica_groups=mesh['net'=128,'scen'=4] {'net'}, use_global_device_ids=true, to_apply=%region_5.8 | all-reduce | flops 64 | bytes 512 | tf_op jit(solution)/shard_map/psum | solution.py:181
  384.8 246.8 %psum.58 = f32[32]{0:T(128)S(1)} all-reduce(f32[32]{0:T(128)S(1)} %multiply_reduce_fusion.5), channel_id=1, replica_groups=mesh['net'=128,'scen'=4] {'net'}, use_global_device_ids=true, to_apply=%region_13.16 | all-reduce | flops 32 | bytes 256 | tf_op jit(solution)/shard_map/psum | solution.py:181
  635.4 7.0 collective-permute-start.9
  646.3 2.0 gather_fusion.11
  649.2 11.9 scatter_fusion.9
  661.3 11.9 scatter_fusion.8
  673.7 7.0 collective-permute-start.10
  683.1 5.0 scatter_fusion.10
  688.1 2.1 collective-permute-done.11
  690.2 5.0 scatter_fusion.11
  695.5 249.9 %psum.59 = f32[32]{0:T(128)S(1)} all-reduce(f32[32]{0:T(128)S(1)} %multiply_reduce_fusion.4), channel_id=1, replica_groups=mesh['net'=128,'scen'=4] {'net'}, use_global_device_ids=true, to_apply=%region_19.22 | all-reduce | flops 32 | bytes 256 | tf_op jit(solution)/shard_map/psum | solution.py:206
  945.6 246.8 %psum.60 = f32[32]{0:T(128)S(1)} all-reduce(f32[32]{0:T(128)S(1)} %multiply_reduce_fusion.3), channel_id=1, replica_groups=mesh['net'=128,'scen'=4] {'net'}, use_global_device_ids=true, to_apply=%region_21.24 | all-reduce | flops 32 | bytes 256 | tf_op jit(solution)/shard_map/psum | solution.py:181
  1196.3 7.2 collective-permute-start.13
  1207.2 2.0 gather_fusion.15
  1210.1 11.9 scatter_fusion.13
  1222.2 11.9 scatter_fusion.12
  1234.5 7.0 collective-permute-start.14
  1243.9 5.0 scatter_fusion.14
  1248.9 2.1 collective-permute-done.15
  1251.0 5.0 scatter_fusion.15
  1256.3 249.9 %psum.61 = f32[32]{0:T(128)S(1)} all-reduce(f32[32]{0:T(128)S(1)} %multiply_reduce_fusion.2), channel_id=1, replica_groups=mesh['net'=128,'scen'=4] {'net'}, use_global_device_ids=true, to_apply=%region_27.30 | all-reduce | flops 32 | bytes 256 | tf_op jit(solution)/shard_map/psum | solution.py:206
  1506.4 246.8 %psum.62 = f32[32]{0:T(128)S(1)} all-reduce(f32[32]{0:T(128)S(1)} %multiply_reduce_fusion.1), channel_id=1, replica_groups=mesh['net'=128,'scen'=4] {'net'}, use_global_device_ids=true, to_apply=%region_29.32 | all-reduce | flops 32 | bytes 256 | tf_op jit(solution)/shard_map/psum | solution.py:181
  1757.1 7.0 collective-permute-start.17
  1768.0 2.0 gather_fusion.19
  1770.9 11.9 scatter_fusion.17
  1783.0 11.9 scatter_fusion.16
  1795.4 7.0 collective-permute-start.18
  1804.8 5.0 scatter_fusion.18
  1809.8 2.1 collective-permute-done.19
  1811.9 5.0 scatter_fusion.19
  1817.2 249.9 %psum.63 = f32[32]{0:T(128)S(1)} all-reduce(f32[32]{0:T(128)S(1)} %multiply_reduce_fusion), channel_id=1, replica_groups=mesh['net'=128,'scen'=4] {'net'}, use_global_device_ids=true, to_apply=%region_35.38 | all-reduce | flops 32 | bytes 256 | tf_op jit(solution)/shard_map/psum | solution.py:206
  (230 shorter events, 63.2 us)
Async XLA Ops:
  0.6 55.1 %copy-start = (f32[40]{0:T(128)S(1)}, f32[40]{0:T(128)}, u32[]{:S(2)}) copy-start(f32[40]{0:T(128)} %param.29) | copy-start | bytes 484
  3.4 11.3 collective-permute-start
  6.0 7.2 copy-start.3
  6.3 9.4 collective-permute-start.1
  13.2 0.7 copy-start.4
  13.9 0.7 copy-start.7
  13.9 0.7 copy-start.8
  20.2 0.9 copy-start.5
  20.2 0.9 copy-start.6
  46.6 9.1 copy-start.9
  46.6 10.8 collective-permute-start.2
  53.8 10.8 collective-permute-start.3
  70.0 0.9 copy-start.1
  70.0 0.9 copy-start.2
  72.6 9.0 collective-permute-start.4
  74.6 8.5 collective-permute-start.5
  112.9 9.4 collective-permute-start.6
  119.9 9.5 collective-permute-start.7
  633.4 9.0 collective-permute-start.8
  635.4 8.5 collective-permute-start.9
  673.7 9.4 collective-permute-start.10
  680.7 9.5 collective-permute-start.11
  1194.3 9.2 collective-permute-start.12
  1196.3 8.5 collective-permute-start.13
  1234.5 9.4 collective-permute-start.14
  1241.5 9.5 collective-permute-start.15
  1755.1 9.0 collective-permute-start.16
  1757.1 8.5 collective-permute-start.17
  1795.4 9.4 collective-permute-start.18
  1802.4 9.5 collective-permute-start.19
where the time goes:
time: 2070 us
  blocking collectives  1740 us (84%)
  other arithmetic  177 us (9%)
  starting transfers between devices  89.4 us (4%)
  local copies, waits for them, and re-layouts  38.9 us (2%)
    psum x4, blocking collectives, energy_of(): return lax.psum(scenario_sum(residual_now, scaled_now), 'net')  990 us
    psum x3, blocking collectives, body(): step_size = energy / lax.psum(scenario_sum(search, local_sum), 'net')  750 us
    ppermute x20, starting transfers between devices, shifted(): return lax.ppermute(array, axis, pairs)  89.4 us
    scatter-add x4, other arithmetic, body(): jax.ops.segment_sum(to_terms, branch_to, num_segments=extended_size)  47.8 us
    scatter-add x4, other arithmetic, body(): jax.ops.segment_sum(from_terms, branch_from, num_segments=extended_size)  47.8 us
  transfers between devices with their start and end apart: 20, of which 15 were waited for; matrix products, arithmetic and copies ran while one was open for 1% of the time, Pallas kernels for 0%

commit v1 on v0

v1 whole, which is shorter than its diff:
```python
import functools

import jax
import jax.numpy as jnp
from jax import lax
from jax.experimental import pallas as pl
from jax.experimental.pallas import tpu as pltpu
from jax.sharding import PartitionSpec as P

MESH = pl.DeviceIdType.MESH
F32, BF16 = jnp.float32, jnp.bfloat16
ITERS = 4
LANES = 128

barrier_weight = 0.01
volt_low = 0.9
volt_high = 1.1
angle_reg = 0.5


def sine_cosine(angle):
    square = angle * angle
    sine = 1.0 / 6227020800.0
    for term in (-1.0 / 39916800.0, 1.0 / 362880.0, -1.0 / 5040.0, 1.0 / 120.0, -1.0 / 6.0, 1.0):
        sine = sine * square + term
    cosine = -1.0 / 87178291200.0
    for term in (1.0 / 479001600.0, -1.0 / 3628800.0, 1.0 / 40320.0, -1.0 / 720.0, 1.0 / 24.0, -0.5, 1.0):
        cosine = cosine * square + term
    return sine * angle, cosine


def branch_blocks(mag_from, mag_to, sine, cosine, conduct, suscept, weight_p, weight_q):
    along = conduct * cosine + suscept * sine
    across = conduct * sine - suscept * cosine
    cross = mag_from * mag_to
    jp = (2.0 * conduct * mag_from - mag_to * along, cross * across, -mag_from * along, -cross * across)
    jq = (-2.0 * suscept * mag_from - mag_to * across, -cross * along, -mag_from * across, cross * along)
    wp = [weight_p * j for j in jp]
    wq = [weight_q * j for j in jq]

    def entry(i, j):
        return wp[i] * jp[j] + wq[i] * jq[j]

    return (
        (entry(0, 0), entry(0, 1), entry(1, 1)),
        (entry(2, 2), entry(2, 3), entry(3, 3)),
        (entry(0, 2), entry(0, 3), entry(1, 2), entry(1, 3)),
    )


def pieces(values, terms):
    out = []
    for _ in range(terms - 1):
        head = values.astype(BF16)
        out.append(head)
        values = values - head.astype(F32)
    return jnp.concatenate(out + [values.astype(BF16)], axis=0)


def select_dot(values, table, terms):
    rows = values.shape[0]
    out = jnp.dot(pieces(values, terms), table, preferred_element_type=F32)
    total = out[(terms - 1) * rows :]
    for k in range(terms - 2, -1, -1):
        total = total + out[k * rows : (k + 1) * rows]
    return total


def inner(left, right):
    product = left * right
    half = product.shape[0] // 2
    product = product[:half] + product[half:]
    product = product[:, :LANES] + product[:, LANES:]
    return jnp.sum(product, axis=1, keepdims=True)


def pack(sums):
    lane = lax.broadcasted_iota(jnp.int32, (8, LANES), 1)
    tile = jnp.zeros((8, LANES), F32)
    for m, column in enumerate(sums):
        for g in range(4):
            tile = jnp.where(lane == 4 * m + g, column[8 * g : 8 * g + 8], tile)
    return tile


def unpack(tile):
    return jnp.concatenate([tile[:, g : g + 1] for g in range(4)], axis=0)


def galerkin(gram, rhs, n):
    a = {(i, j): gram[(min(i, j), max(i, j))] for i in range(n) for j in range(n)}
    rhs = list(rhs)
    low, inv = {}, {}
    for k in range(n):
        live = a[(k, k)] > 1e-7 * gram[(k, k)]
        inv[k] = jnp.where(live, 1.0 / jnp.where(live, a[(k, k)], 1.0), 0.0)
        for i in range(k + 1, n):
            low[(i, k)] = a[(i, k)] * inv[k]
            for j in range(k + 1, i + 1):
                a[(i, j)] = a[(i, j)] - low[(i, k)] * a[(j, k)]
                a[(j, i)] = a[(i, j)]
            rhs[i] = rhs[i] - low[(i, k)] * rhs[k]
    out = [None] * n
    for k in reversed(range(n)):
        value = rhs[k] * inv[k]
        for i in range(k + 1, n):
            value = value - low[(i, k)] * out[i]
        out[k] = value
    return out


def kernel(
    n,
    group,
    vm_ref,
    va_ref,
    grad_ref,
    from_ref,
    to_ref,
    count_ref,
    bound_ref,
    g_ref,
    b_ref,
    dual_ref,
    slack_ref,
    gbus_ref,
    gcur_ref,
    x_ref,
    r_ref,
    irow,
    frow,
    vin,
    gather_tab,
    scatter_tab,
    pay_out,
    pay_in,
    halo_out,
    halo_in,
    red_a,
    red_b,
    pay_send,
    pay_recv,
    halo_send,
    halo_recv,
    a_send,
    a_recv,
    b_send,
    b_recv,
):
    scen, buses = vm_ref.shape
    slots = from_ref.shape[1]
    ghost = buses // 2
    wide = 2 * LANES
    span = gather_tab.shape[1] // 2
    gens = gbus_ref.shape[1]
    outer = n // group
    me = lax.axis_index("net")
    prev, nxt = lax.rem(me + n - 1, n), lax.rem(me + 1, n)
    inside = lax.rem(me, group)
    block = lax.div(me, group)
    peers_a = [block * group + lax.rem(inside + d, group) for d in range(1, group)]
    peers_b = [lax.rem(block + d, outer) * group + inside for d in range(1, outer)]

    barrier = pltpu.get_barrier_semaphore()
    for peer in (prev, nxt, *peers_a, *peers_b):
        pl.semaphore_signal(barrier, inc=1, device_id={"net": peer}, device_id_type=MESH)

    def exchange(source, target, send, recv):
        out = []
        for half, peer in ((0, prev), (1, nxt)):
            copy = pltpu.make_async_remote_copy(
                src_ref=source.at[half],
                dst_ref=target.at[1 - half],
                send_sem=send.at[half],
                recv_sem=recv.at[half],
                device_id={"net": peer},
                device_id_type=MESH,
            )
            copy.start()
            out.append(copy)
        return out

    irow[...] = jnp.full(irow.shape, -1.0, F32)
    irow[0:1, :slots] = from_ref[...].astype(F32)
    irow[1:2, :slots] = to_ref[...].astype(F32)
    irow[2:3, :buses] = bound_ref[...].astype(F32)
    irow[3:4, :gens] = gbus_ref[...].astype(F32)
    frow[...] = jnp.zeros(frow.shape, F32)
    frow[0:1, :slots] = g_ref[...]
    frow[1:2, :slots] = b_ref[...]
    frow[2:3, :gens] = gcur_ref[...]
    from_row, to_row = irow[0:1, :], irow[1:2, :]
    lane_i = lax.broadcasted_iota(jnp.int32, (8, wide), 1)
    lane = lane_i.astype(F32)
    plain = irow[0:8, :wide]
    rolled = pltpu.roll(plain, LANES - ghost, 1)
    upper = (lane_i >= LANES) & (lane_i < LANES + ghost)
    place = jnp.where(lane_i < ghost, plain, jnp.where(upper, rolled, -2.0))[2:3]
    entry = jnp.where(lane_i < ghost, lane, jnp.where(upper, lane - (LANES - ghost), -1e6))[0:1]

    def column(row):
        return jnp.transpose(jnp.broadcast_to(row, (LANES, row.shape[1])))

    def hot(mask):
        return jnp.where(mask, 1.0, 0.0).astype(BF16)

    place_col, from_col, to_col = column(place), column(from_row), column(to_row)
    lanes_of = lambda row, t: row[:, t * LANES : (t + 1) * LANES]
    for t in range(span // LANES):
        gather_tab[:, t * LANES : (t + 1) * LANES] = hot(place_col == lanes_of(from_row, t))
        gather_tab[:, span + t * LANES : span + (t + 1) * LANES] = hot(place_col == lanes_of(to_row, t))
    for t in range(2):
        cols = slice(t * LANES, (t + 1) * LANES)
        scatter_tab[0:span, cols] = hot(from_col == lanes_of(place, t))
        scatter_tab[span:, cols] = hot(to_col == lanes_of(place, t))
    cross_tab = jnp.concatenate([hot(to_col == lanes_of(entry, t) + buses) for t in range(2)], axis=1)
    bus_row = lane[0:1]
    bus_col = lax.broadcasted_iota(jnp.int32, (wide, LANES), 0).astype(F32)
    to_place = jnp.concatenate([hot(bus_col == lanes_of(place, t)) for t in range(2)], axis=1)
    to_bus = jnp.concatenate([hot(place_col == lanes_of(bus_row, t)) for t in range(2)], axis=1)

    vin[...] = jnp.zeros(vin.shape, F32)
    vin[0:scen, :buses] = vm_ref[...]
    vin[scen : 2 * scen, :buses] = va_ref[...]
    vin[2 * scen : 3 * scen, :buses] = grad_ref[0]
    vin[3 * scen : 4 * scen, :buses] = grad_ref[1]
    placed = select_dot(vin[...], to_place, 3)
    vm, va, start = placed[0:scen], placed[scen : 2 * scen], placed[2 * scen :]

    slot = lax.broadcasted_iota(jnp.int32, (1, slots), 1)
    live = jnp.where(slot < count_ref[...], 1.0, 0.0)
    pad = jnp.zeros((scen, span - slots), F32)
    weight_p = jnp.concatenate([live * dual_ref[0] / slack_ref[0], pad], axis=1)
    weight_q = jnp.concatenate([live * dual_ref[1] / slack_ref[1], pad], axis=1)
    conduct, suscept = frow[0:1, :], frow[1:2, :]
    stacked = jnp.concatenate([weight_p, weight_q, frow[0:8, :]], axis=0)
    crossing = select_dot(stacked, cross_tab, 3)
    payload = jnp.concatenate([vm, va, crossing], axis=0)
    for half in range(2):
        pay_out[half] = payload[:, half * LANES : (half + 1) * LANES]

    pl.semaphore_wait(barrier, 2 + (group - 1) + (outer - 1))
    pay_copies = exchange(pay_out, pay_in, pay_send, pay_recv)

    ends = select_dot(placed[0 : 2 * scen], gather_tab[...], 3)
    local = jnp.where((to_row >= 0.0) & (to_row < float(buses)), 1.0, 0.0)
    sine, cosine = sine_cosine(ends[scen:, :span] - ends[scen:, span:])
    hff, htt, (h00, h01, h10, h11) = branch_blocks(
        ends[:scen, :span], ends[:scen, span:], sine, cosine, conduct, suscept, weight_p * local, weight_q * local
    )
    both = jnp.concatenate([jnp.concatenate([a, b], axis=1) for a, b in zip(hff, htt)], axis=0)
    diag = select_dot(both, scatter_tab[...], 3)
    gen = column(irow[3:4, :LANES])
    curve = column(frow[2:3, :LANES])
    gen_sum = jnp.concatenate(
        [jnp.sum(jnp.where(gen == lanes_of(place, t), curve, 0.0), axis=0, keepdims=True) for t in range(2)], axis=1
    )
    low, high = vm - volt_low, volt_high - vm
    base_vv = barrier_weight / (low * low) + barrier_weight / (high * high) + gen_sum
    base_aa = angle_reg + gen_sum

    for copy in pay_copies:
        copy.wait()
    arrived = jnp.concatenate([pay_in[0], pay_in[1]], axis=1)
    there_vm, there_va = arrived[0:scen], arrived[scen : 2 * scen]
    there_p, there_q = arrived[2 * scen : 3 * scen], arrived[3 * scen : 4 * scen]
    there_g, there_b = arrived[4 * scen : 4 * scen + 1], arrived[4 * scen + 1 : 4 * scen + 2]
    here_p, here_q = crossing[0:scen], crossing[scen : 2 * scen]
    here_g, here_b = crossing[2 * scen : 2 * scen + 1], crossing[2 * scen + 1 : 2 * scen + 2]
    sine, cosine = sine_cosine(va - there_va)
    off, _, (o00, o01, o10, o11) = branch_blocks(vm, there_vm, sine, cosine, here_g, here_b, here_p, here_q)
    _, on, (i00, i01, i10, i11) = branch_blocks(there_vm, vm, -sine, cosine, there_g, there_b, there_p, there_q)
    c00, c01, c10, c11 = o00 + i00, o01 + i10, o10 + i01, o11 + i11
    d00 = diag[0:scen] + off[0] + on[0] + base_vv
    d01 = diag[scen : 2 * scen] + off[1] + on[1]
    d11 = diag[2 * scen :] + off[2] + on[2] + base_aa
    inverse = 1.0 / (d00 * d11 - d01 * d01)
    p00, p01, p11 = d11 * inverse, -d01 * inverse, d00 * inverse

    def precondition(v):
        return jnp.concatenate([p00 * v[:scen] + p01 * v[scen:], p01 * v[:scen] + p11 * v[scen:]], axis=0)

    s, u = [start], [precondition(start)]
    for j in range(ITERS):
        v = u[j]
        halo_out[j, 0] = v[:, :LANES]
        halo_out[j, 1] = v[:, LANES:]
        copies = exchange(halo_out.at[j], halo_in.at[j], halo_send.at[j], halo_recv.at[j])
        ends = select_dot(v, gather_tab[...], 2)
        f0, f1, t0, t1 = ends[:scen, :span], ends[scen:, :span], ends[:scen, span:], ends[scen:, span:]
        terms = jnp.concatenate(
            [
                jnp.concatenate([h00 * t0 + h01 * t1, h00 * f0 + h10 * f1], axis=1),
                jnp.concatenate([h10 * t0 + h11 * t1, h01 * f0 + h11 * f1], axis=1),
            ],
            axis=0,
        )
        inside_sum = select_dot(terms, scatter_tab[...], 2)
        for copy in copies:
            copy.wait()
        n0 = jnp.concatenate([halo_in[j, 0, :scen], halo_in[j, 1, :scen]], axis=1)
        n1 = jnp.concatenate([halo_in[j, 0, scen:], halo_in[j, 1, scen:]], axis=1)
        s.append(inside_sum + jnp.concatenate([c00 * n0 + c01 * n1, c10 * n0 + c11 * n1], axis=0))
        if j + 1 < ITERS:
            u.append(precondition(s[-1]))

    def all_sum(tile):
        red_a[pl.ds(inside, 1)] = tile[None]
        copies = []
        for d, peer in enumerate(peers_a):
            copy = pltpu.make_async_remote_copy(
                src_ref=red_a.at[inside],
                dst_ref=red_a.at[inside],
                send_sem=a_send.at[d],
                recv_sem=a_recv.at[d],
                device_id={"net": peer},
                device_id_type=MESH,
            )
            copy.start()
            copies.append(copy)
        for copy in copies:
            copy.wait()
        total = red_a[0]
        for k in range(1, group):
            total = total + red_a[k]
        red_b[pl.ds(block, 1)] = total[None]
        copies = []
        for d, peer in enumerate(peers_b):
            copy = pltpu.make_async_remote_copy(
                src_ref=red_b.at[block],
                dst_ref=red_b.at[block],
                send_sem=b_send.at[d],
                recv_sem=b_recv.at[d],
                device_id={"net": peer},
                device_id_type=MESH,
            )
            copy.start()
            copies.append(copy)
        for copy in copies:
            copy.wait()
        total = red_b[0]
        for k in range(1, outer):
            total = total + red_b[k]
        return total

    total = all_sum(pack([inner(u[k // 2], s[k - k // 2]) for k in range(2 * ITERS)]))
    moments = [total] + [pltpu.roll(total, LANES - 4 * m, 1) for m in range(1, 2 * ITERS)]
    gram = {(i, j): moments[i + j] + moments[i + j + 1] for i in range(ITERS) for j in range(i, ITERS)}
    weights = galerkin(gram, moments[:ITERS], ITERS)
    weights = [unpack(w) for w in weights]
    weights = [jnp.concatenate([w, w], axis=0) for w in weights]
    step = weights[0] * u[0]
    residual = s[0] - weights[0] * (s[0] + s[1])
    for j in range(1, ITERS):
        step = step + weights[j] * u[j]
        residual = residual - weights[j] * (s[j] + s[j + 1])
    out = select_dot(jnp.concatenate([step, residual], axis=0), to_bus, 3)
    for c in range(2):
        x_ref[c] = out[c * scen : (c + 1) * scen, :buses]
        r_ref[c] = out[(2 + c) * scen : (3 + c) * scen, :buses]


def body(
    n,
    volt_mag,
    volt_ang,
    gradient,
    branch_from,
    branch_to,
    branch_count,
    boundary,
    conductance,
    susceptance,
    duals,
    slacks,
    gen_bus,
    gen_curvature,
):
    buses, scen = volt_mag.shape
    slots = branch_from.shape[0]
    span = -(-slots // LANES) * LANES
    group = 16 if n % 16 == 0 and n > 16 else 4 if n % 4 == 0 else 1
    outer = n // group
    row = lambda a: a.reshape(1, -1)
    rows = 4 * scen + 8
    dma = lambda *shape: pltpu.SemaphoreType.DMA(shape)
    step, residual = pl.pallas_call(
        functools.partial(kernel, n, group),
        out_shape=[jax.ShapeDtypeStruct((2, scen, buses), F32)] * 2,
        in_specs=[pl.BlockSpec(memory_space=pltpu.VMEM)] * 13,
        out_specs=[pl.BlockSpec(memory_space=pltpu.VMEM)] * 2,
        scratch_shapes=[
            pltpu.VMEM((8, span), F32),
            pltpu.VMEM((8, span), F32),
            pltpu.VMEM((4 * scen, 2 * LANES), F32),
            pltpu.VMEM((2 * LANES, 2 * span), BF16),
            pltpu.VMEM((2 * span, 2 * LANES), BF16),
            pltpu.VMEM((2, rows, LANES), F32),
            pltpu.VMEM((2, rows, LANES), F32),
            pltpu.VMEM((ITERS, 2, 2 * scen, LANES), F32),
            pltpu.VMEM((ITERS, 2, 2 * scen, LANES), F32),
            pltpu.VMEM((group, 8, LANES), F32),
            pltpu.VMEM((outer, 8, LANES), F32),
            dma(2),
            dma(2),
            dma(ITERS, 2),
            dma(ITERS, 2),
            dma(group),
            dma(group),
            dma(outer),
            dma(outer),
        ],
        compiler_params=pltpu.CompilerParams(
            collective_id=0, has_side_effects=True, vmem_limit_bytes=32 * 1024 * 1024
        ),
        name="newton",
    )(
        volt_mag.T,
        volt_ang.T,
        gradient.transpose(1, 2, 0),
        row(branch_from),
        row(branch_to),
        row(branch_count),
        row(boundary),
        row(conductance),
        row(susceptance),
        duals.transpose(0, 2, 1),
        slacks.transpose(0, 2, 1),
        row(gen_bus),
        row(gen_curvature),
    )
    return step.transpose(2, 0, 1), residual.transpose(2, 0, 1)


def solution(mesh):
    placed = (
        P("net", "scen"),
        P("net", "scen"),
        P("net", None, "scen"),
        P("net"),
        P("net"),
        P("net"),
        P("net"),
        P("net"),
        P("net"),
        P(None, "net", "scen"),
        P(None, "net", "scen"),
        P("net"),
        P("net"),
    )
    return jax.shard_map(
        functools.partial(body, mesh.shape["net"]),
        mesh=mesh,
        in_specs=placed,
        out_specs=(P("net", None, "scen"), P("net", None, "scen")),
        check_vma=False,
    )
```

time: 2070 us -> 52.7 us (0.03)
  the two profiles are of different devices: /device:TPU:258 before, /device:TPU:1 now
where the time goes in v1:
time: 52.7 us; the launch traced here: 52.3 us
  Pallas kernels  42.2 us (80%)
  local copies, waits for them, and re-layouts  8.73 us (17%)
  between operations  1.31 us (2%)
    pallas_call x1, Pallas kernels, body(): pl.pallas_call(functools.partial(kernel, n, group), out_shape=[jax.ShapeD...  42.2 us
    unnamed x18, local copies, waits for them, and re-layouts  5.98 us
    reshape x4, local copies, waits for them, and re-layouts, body(): row = lambda a: a.reshape(1, -1)  2.75 us

profile of v1, /device:TPU:1, one launch (start us, length us, event | category | flops | bytes accessed | tf_op | source)
XLA Modules:
  0.0 52.3 jit_solution(1094458604363737298)
XLA Ops:
  0.6 0.0 copy-start.3
  1.3 0.7 %reshape.28.from_ref = s32[1,320]{1,0:T(1,128)S(1)} reshape(s32[320]{0:T(512)} %param.16) | data formatting | bytes 2560 | tf_op jit(solution)/shard_map/reshape | solution.py:384
  2.0 0.7 %reshape.29.to_ref = s32[1,320]{1,0:T(1,128)S(1)} reshape(s32[320]{0:T(512)} %param.17) | data formatting | bytes 2560 | tf_op jit(solution)/shard_map/reshape | solution.py:384
  2.7 0.7 %reshape.32.g_ref = f32[1,320]{1,0:T(1,128)S(1)} reshape(f32[320]{0:T(512)} %param.20) | data formatting | bytes 2560 | tf_op jit(solution)/shard_map/reshape | solution.py:384
  3.3 0.0 copy-start.6
  3.3 0.7 %reshape.33.b_ref = f32[1,320]{1,0:T(1,128)S(1)} reshape(f32[320]{0:T(512)} %param.21) | data formatting | bytes 2560 | tf_op jit(solution)/shard_map/reshape | solution.py:384
  4.0 0.0 copy-done.3
  4.0 0.0 copy-done.6
  4.0 0.0 copy-start
  4.1 0.9 %copy-done = f32[2,320,32]{1,2,0:T(8,128)S(1)} copy-done((f32[2,320,32]{1,2,0:T(8,128)S(1)}, f32[2,320,32]{1,2,0:T(8,128)}, u32[]{:S(2)}) %copy-start) | copy-done | bytes 81944
  4.9 0.0 copy-start.1
  4.9 0.9 %copy-done.1 = f32[2,320,32]{1,2,0:T(8,128)S(1)} copy-done((f32[2,320,32]{1,2,0:T(8,128)S(1)}, f32[2,320,32]{1,2,0:T(8,128)}, u32[]{:S(2)}) %copy-start.1) | copy-done | bytes 81944
  5.8 0.0 copy-start.2
  5.8 0.8 %copy-done.2 = f32[240,2,32]{0,2,1:T(8,128)S(1)} copy-done((f32[240,2,32]{0,2,1:T(8,128)S(1)}, f32[240,2,32]{0,2,1:T(8,128)}, u32[]{:S(2)}) %copy-start.2) | copy-done | bytes 61464
  6.7 0.0 copy-start.4
  6.7 0.8 %copy-done.4 = f32[240,32]{0,1:T(8,128)S(1)} copy-done((f32[240,32]{0,1:T(8,128)S(1)}, f32[240,32]{0,1:T(8,128)}, u32[]{:S(2)}) %copy-start.4) | copy-done | bytes 30744
  7.4 0.0 copy-start.5
  7.4 0.7 %copy-done.5 = s32[240]{0:T(256)S(1)} copy-done((s32[240]{0:T(256)S(1)}, s32[240]{0:T(256)}, u32[]{:S(2)}) %copy-start.5) | copy-done | bytes 984
  8.1 0.0 copy-start.7
  8.1 0.7 %copy-done.7 = f32[40]{0:T(128)S(1)} copy-done((f32[40]{0:T(128)S(1)}, f32[40]{0:T(128)}, u32[]{:S(2)}) %copy-start.7) | copy-done | bytes 184
  8.8 42.2 %newton.1 = (f32[2,32,240]{2,1,0:T(8,128)S(1)}, f32[2,32,240]{2,1,0:T(8,128)S(1)}) custom-call(f32[32,240]{1,0:T(8,128)S(1)} %bitcast.17, f32[32,240]{1,0:T(8,128)S(1)} %bitcast.18, f32[2,32,240]{2,1,0:T(8,128)S(1)} %bitcast.16, s32[1,320]{1,0:T(1,128)S(1)} %reshape.28.from_ref, s32[1,320]{1,0:T(1,128)S(1)} %reshape.29.to_ref, s32[1,1]{1,0:T(1,128)} %bitcast.11.count_ref, ...), custom_call_target="tpu_custom_call" | custom-call | tf_op jit(solution)/shard_map/newton/pallas_call | solution.py:387
  51.0 0.6 %copy.18 = f32[240,2,32]{0,2,1:T(8,128)} copy(f32[240,2,32]{0,2,1:T(8,128)S(1)} %bitcast.15) | data formatting | bytes 122880
  51.6 0.6 %copy.19 = f32[240,2,32]{0,2,1:T(8,128)} copy(f32[240,2,32]{0,2,1:T(8,128)S(1)} %bitcast.14) | data formatting | bytes 122880
Async XLA Ops:
  0.6 3.4 %copy-start.3 = (f32[240,32]{0,1:T(8,128)S(1)}, f32[240,32]{0,1:T(8,128)}, u32[]{:S(2)}) copy-start(f32[240,32]{0,1:T(8,128)} %param.13) | copy-start | bytes 92164
  3.3 0.7 %copy-start.6 = (s32[40]{0:T(128)S(1)}, s32[40]{0:T(128)}, u32[]{:S(2)}) copy-start(s32[40]{0:T(128)} %param.24) | copy-start | bytes 484
  4.0 0.9 %copy-start = (f32[2,320,32]{1,2,0:T(8,128)S(1)}, f32[2,320,32]{1,2,0:T(8,128)}, u32[]{:S(2)}) copy-start(f32[2,320,32]{1,2,0:T(8,128)} %param.22) | copy-start | bytes 245764
  4.9 0.9 %copy-start.1 = (f32[2,320,32]{1,2,0:T(8,128)S(1)}, f32[2,320,32]{1,2,0:T(8,128)}, u32[]{:S(2)}) copy-start(f32[2,320,32]{1,2,0:T(8,128)} %param.23) | copy-start | bytes 245764
  5.8 0.8 %copy-start.2 = (f32[240,2,32]{0,2,1:T(8,128)S(1)}, f32[240,2,32]{0,2,1:T(8,128)}, u32[]{:S(2)}) copy-start(f32[240,2,32]{0,2,1:T(8,128)} %param.15) | copy-start | bytes 184324
  6.7 0.8 %copy-start.4 = (f32[240,32]{0,1:T(8,128)S(1)}, f32[240,32]{0,1:T(8,128)}, u32[]{:S(2)}) copy-start(f32[240,32]{0,1:T(8,128)} %param.14) | copy-start | bytes 92164
  7.4 0.7 %copy-start.5 = (s32[240]{0:T(256)S(1)}, s32[240]{0:T(256)}, u32[]{:S(2)}) copy-start(s32[240]{0:T(256)} %param.19) | copy-start | bytes 2884
  8.1 0.7 %copy-start.7 = (f32[40]{0:T(128)S(1)}, f32[40]{0:T(128)}, u32[]{:S(2)}) copy-start(f32[40]{0:T(128)} %param.25) | copy-start | bytes 484

commit v2 on v1

--- a/solution.py
+++ b/solution.py
@@ -112,6 +112,22 @@
 def kernel(
     n,
     group,
+    *refs,
+):
+    inputs, (x_ref, r_ref), loaded, rest = refs[:13], refs[13:15], refs[15:28], refs[28:]
+    load_sem = rest[0]
+    loads = []
+    for k, (source, target) in enumerate(zip(inputs, loaded)):
+        copy = pltpu.make_async_copy(source, target, load_sem.at[k])
+        copy.start()
+        loads.append(copy)
+    solve(n, group, loads, *loaded, x_ref, r_ref, *rest[1:])
+
+
+def solve(
+    n,
+    group,
+    loads,
     vm_ref,
     va_ref,
     grad_ref,
@@ -148,7 +164,7 @@
     b_recv,
 ):
     scen, buses = vm_ref.shape
-    slots = from_ref.shape[1]
+    slots = from_ref.shape[-1]
     ghost = buses // 2
     wide = 2 * LANES
     span = gather_tab.shape[1] // 2
@@ -180,14 +196,17 @@
             out.append(copy)
         return out
 
+    for copy in loads:
+        copy.wait()
+
     irow[...] = jnp.full(irow.shape, -1.0, F32)
-    irow[0:1, :slots] = from_ref[...].astype(F32)
-    irow[1:2, :slots] = to_ref[...].astype(F32)
+    irow[0:1, :slots] = from_ref[...].reshape(1, slots).astype(F32)
+    irow[1:2, :slots] = to_ref[...].reshape(1, slots).astype(F32)
     irow[2:3, :buses] = bound_ref[...].astype(F32)
     irow[3:4, :gens] = gbus_ref[...].astype(F32)
     frow[...] = jnp.zeros(frow.shape, F32)
-    frow[0:1, :slots] = g_ref[...]
-    frow[1:2, :slots] = b_ref[...]
+    frow[0:1, :slots] = g_ref[...].reshape(1, slots)
+    frow[1:2, :slots] = b_ref[...].reshape(1, slots)
     frow[2:3, :gens] = gcur_ref[...]
     from_row, to_row = irow[0:1, :], irow[1:2, :]
     lane_i = lax.broadcasted_iota(jnp.int32, (8, wide), 1)
@@ -228,7 +247,7 @@
     vm, va, start = placed[0:scen], placed[scen : 2 * scen], placed[2 * scen :]
 
     slot = lax.broadcasted_iota(jnp.int32, (1, slots), 1)
-    live = jnp.where(slot < count_ref[...], 1.0, 0.0)
+    live = jnp.where(slot < count_ref[...].reshape(1, 1), 1.0, 0.0)
     pad = jnp.zeros((scen, span - slots), F32)
     weight_p = jnp.concatenate([live * dual_ref[0] / slack_ref[0], pad], axis=1)
     weight_q = jnp.concatenate([live * dual_ref[1] / slack_ref[1], pad], axis=1)
@@ -384,12 +403,29 @@
     row = lambda a: a.reshape(1, -1)
     rows = 4 * scen + 8
     dma = lambda *shape: pltpu.SemaphoreType.DMA(shape)
+    operands = (
+        volt_mag.T,
+        volt_ang.T,
+        gradient.transpose(1, 2, 0),
+        branch_from,
+        branch_to,
+        branch_count,
+        row(boundary),
+        conductance,
+        susceptance,
+        duals.transpose(0, 2, 1),
+        slacks.transpose(0, 2, 1),
+        row(gen_bus),
+        row(gen_curvature),
+    )
     step, residual = pl.pallas_call(
         functools.partial(kernel, n, group),
         out_shape=[jax.ShapeDtypeStruct((2, scen, buses), F32)] * 2,
-        in_specs=[pl.BlockSpec(memory_space=pltpu.VMEM)] * 13,
+        in_specs=[pl.BlockSpec(memory_space=pltpu.HBM)] * 13,
         out_specs=[pl.BlockSpec(memory_space=pltpu.VMEM)] * 2,
         scratch_shapes=[
+            *(pltpu.VMEM(a.shape, a.dtype) for a in operands),
+            dma(13),
             pltpu.VMEM((8, span), F32),
             pltpu.VMEM((8, span), F32),
             pltpu.VMEM((4 * scen, 2 * LANES), F32),
@@ -411,24 +447,10 @@
             dma(outer),
         ],
         compiler_params=pltpu.CompilerParams(
-            collective_id=0, has_side_effects=True, vmem_limit_bytes=32 * 1024 * 1024
+            collective_id=0, has_side_effects=True, vmem_limit_bytes=62 * 1024 * 1024
         ),
         name="newton",
-    )(
-        volt_mag.T,
-        volt_ang.T,
-        gradient.transpose(1, 2, 0),
-        row(branch_from),
-        row(branch_to),
-        row(branch_count),
-        row(boundary),
-        row(conductance),
-        row(susceptance),
-        duals.transpose(0, 2, 1),
-        slacks.transpose(0, 2, 1),
-        row(gen_bus),
-        row(gen_curvature),
-    )
+    )(*operands)
     return step.transpose(2, 0, 1), residual.transpose(2, 0, 1)
 
 

time: 52.7 us -> 46.6 us (0.88)
  local copies, waits for them, and re-layouts: 8.73 us -> 2.14 us
  Pallas kernels: 42.2 us -> 43 us
    unnamed x18 -> x4, local copies, waits for them, and re-layouts: 5.98 us -> 2.14 us
    reshape x4 -> x0, local copies, waits for them, and re-layouts: 2.75 us -> none  [body(): row = lambda a: a.reshape(1, -1)]
    pallas_call x1, Pallas kernels: 42.2 us -> 43 us  [body(): pl.pallas_call(functools.partial(kernel, n, group), out_shape=[jax.ShapeD...]
where the time goes in v2:
time: 46.6 us; the launch traced here: 46.4 us
  Pallas kernels  43 us (92%)
  local copies, waits for them, and re-layouts  2.14 us (5%)
  between operations  1.3 us (3%)
    pallas_call x1, Pallas kernels, body(): pl.pallas_call(functools.partial(kernel, n, group), out_shape=[jax.ShapeD...  43 us
    unnamed x4, local copies, waits for them, and re-layouts  2.14 us

profile of v2, /device:TPU:1, one launch (start us, length us, event | category | flops | bytes accessed | tf_op | source)
XLA Modules:
  0.0 46.4 jit_solution(9192903794637171972)
XLA Ops:
  1.3 43.0 %newton.1 = (f32[2,32,240]{2,1,0:T(8,128)}, f32[2,32,240]{2,1,0:T(8,128)}) custom-call(f32[32,240]{1,0:T(8,128)} %bitcast.15, f32[32,240]{1,0:T(8,128)} %bitcast.16, f32[2,32,240]{2,1,0:T(8,128)} %bitcast.14, s32[320]{0:T(512)} %refs_3_.1, s32[320]{0:T(512)} %refs_4_.1, s32[1]{0:T(128)S(6)} %copy.17.refs_5_, s32[1,240]{1,0:T(1,128)} %bitcast.17, ...), custom_call_target="tpu_custom_call" | custom-call | tf_op jit(solution)/shard_map/newton/pallas_call | solution.py:421
  44.3 0.0 copy-start
  44.3 1.5 %copy.18 = f32[240,2,32]{0,2,1:T(8,128)} copy(f32[240,2,32]{0,2,1:T(8,128)} %bitcast.13) | data formatting | bytes 122880
  45.8 0.0 copy-done
  45.8 0.6 %copy.19 = f32[240,2,32]{0,2,1:T(8,128)} copy(f32[240,2,32]{0,2,1:T(8,128)S(1)} %bitcast.12) | data formatting | bytes 122880
Async XLA Ops:
  44.3 1.5 %copy-start = (f32[2,32,240]{2,1,0:T(8,128)S(1)}, f32[2,32,240]{2,1,0:T(8,128)}, u32[]{:S(2)}) copy-start(f32[2,32,240]{2,1,0:T(8,128)} %get-tuple-element.5) | copy-start | bytes 184324

commit v3 on v2

--- a/solution.py
+++ b/solution.py
@@ -70,21 +70,20 @@
     product = left * right
     half = product.shape[0] // 2
     product = product[:half] + product[half:]
-    product = product[:, :LANES] + product[:, LANES:]
-    return jnp.sum(product, axis=1, keepdims=True)
-
-
-def pack(sums):
-    lane = lax.broadcasted_iota(jnp.int32, (8, LANES), 1)
-    tile = jnp.zeros((8, LANES), F32)
-    for m, column in enumerate(sums):
-        for g in range(4):
-            tile = jnp.where(lane == 4 * m + g, column[8 * g : 8 * g + 8], tile)
-    return tile
-
-
-def unpack(tile):
-    return jnp.concatenate([tile[:, g : g + 1] for g in range(4)], axis=0)
+    return product[:, :LANES] + product[:, LANES:]
+
+
+def pack(parts):
+    return jnp.sum(jnp.transpose(jnp.concatenate(parts, axis=0)), axis=0, keepdims=True)
+
+
+def unpack(rows):
+    lane = lax.broadcasted_iota(jnp.int32, (1, LANES), 1)
+    joined = rows[0]
+    for k in range(1, len(rows)):
+        joined = jnp.where(lane < 32 * k, joined, pltpu.roll(rows[k], 32 * k, 1))
+    columns = jnp.transpose(jnp.broadcast_to(joined, (LANES, LANES)))
+    return [columns[32 * k : 32 * k + 32] for k in range(len(rows))]
 
 
 def galerkin(gram, rhs, n):
@@ -114,8 +113,13 @@
     group,
     *refs,
 ):
-    inputs, (x_ref, r_ref), loaded, rest = refs[:13], refs[13:15], refs[15:28], refs[28:]
+    inputs, o_ref, loaded, rest = refs[:13], refs[13], refs[14:27], refs[27:]
+    x_ref, r_ref = o_ref.at[0], o_ref.at[1]
     load_sem = rest[0]
+    me = lax.axis_index("net")
+    neighbours = (lax.rem(me + n - 1, n), lax.rem(me + 1, n))
+    for peer in neighbours:
+        pl.semaphore_signal(pltpu.get_barrier_semaphore(), inc=1, device_id={"net": peer}, device_id_type=MESH)
     loads = []
     for k, (source, target) in enumerate(zip(inputs, loaded)):
         copy = pltpu.make_async_copy(source, target, load_sem.at[k])
@@ -150,12 +154,16 @@
     scatter_tab,
     pay_out,
     pay_in,
+    diag_out,
+    diag_in,
     halo_out,
     halo_in,
     red_a,
     red_b,
     pay_send,
     pay_recv,
+    diag_send,
+    diag_recv,
     halo_send,
     halo_recv,
     a_send,
@@ -178,7 +186,7 @@
     peers_b = [lax.rem(block + d, outer) * group + inside for d in range(1, outer)]
 
     barrier = pltpu.get_barrier_semaphore()
-    for peer in (prev, nxt, *peers_a, *peers_b):
+    for peer in (*peers_a, *peers_b):
         pl.semaphore_signal(barrier, inc=1, device_id={"net": peer}, device_id_type=MESH)
 
     def exchange(source, target, send, recv):
@@ -278,8 +286,16 @@
     base_vv = barrier_weight / (low * low) + barrier_weight / (high * high) + gen_sum
     base_aa = angle_reg + gen_sum
 
+    own = jnp.concatenate(
+        [diag[0:scen] + base_vv, diag[scen : 2 * scen], diag[2 * scen :] + base_aa, start], axis=0
+    )
+    for half in range(2):
+        diag_out[half] = own[:, half * LANES : (half + 1) * LANES]
+    diag_copies = exchange(diag_out, diag_in, diag_send, diag_recv)
+    pending = [*pay_copies, *diag_copies]
+
     for copy in pay_copies:
-        copy.wait()
+        copy.wait_recv()
     arrived = jnp.concatenate([pay_in[0], pay_in[1]], axis=1)
     there_vm, there_va = arrived[0:scen], arrived[scen : 2 * scen]
     there_p, there_q = arrived[2 * scen : 3 * scen], arrived[3 * scen : 4 * scen]
@@ -287,24 +303,38 @@
     here_p, here_q = crossing[0:scen], crossing[scen : 2 * scen]
     here_g, here_b = crossing[2 * scen : 2 * scen + 1], crossing[2 * scen + 1 : 2 * scen + 2]
     sine, cosine = sine_cosine(va - there_va)
-    off, _, (o00, o01, o10, o11) = branch_blocks(vm, there_vm, sine, cosine, here_g, here_b, here_p, here_q)
-    _, on, (i00, i01, i10, i11) = branch_blocks(there_vm, vm, -sine, cosine, there_g, there_b, there_p, there_q)
+    off, reach, (o00, o01, o10, o11) = branch_blocks(vm, there_vm, sine, cosine, here_g, here_b, here_p, here_q)
+    root, on, (i00, i01, i10, i11) = branch_blocks(there_vm, vm, -sine, cosine, there_g, there_b, there_p, there_q)
     c00, c01, c10, c11 = o00 + i00, o01 + i10, o10 + i01, o11 + i11
-    d00 = diag[0:scen] + off[0] + on[0] + base_vv
-    d01 = diag[scen : 2 * scen] + off[1] + on[1]
-    d11 = diag[2 * scen :] + off[2] + on[2] + base_aa
-    inverse = 1.0 / (d00 * d11 - d01 * d01)
-    p00, p01, p11 = d11 * inverse, -d01 * inverse, d00 * inverse
-
+
+    def inverse_of(fields, first, second):
+        d00, d01, d11 = (fields[k * scen : (k + 1) * scen] + first[k] + second[k] for k in range(3))
+        inverse = 1.0 / (d00 * d11 - d01 * d01)
+        return d11 * inverse, -d01 * inverse, d00 * inverse
+
+    def applied(blocks, v):
+        b00, b01, b11 = blocks
+        return jnp.concatenate([b00 * v[:scen] + b01 * v[scen:], b01 * v[:scen] + b11 * v[scen:]], axis=0)
+
+    diag_inverse = inverse_of(own, off, on)
     def precondition(v):
-        return jnp.concatenate([p00 * v[:scen] + p01 * v[scen:], p01 * v[:scen] + p11 * v[scen:]], axis=0)
+        return applied(diag_inverse, v)
+
+    for copy in diag_copies:
+        copy.wait_recv()
+    beyond = jnp.concatenate([diag_in[0], diag_in[1]], axis=1)
+    facing = applied(inverse_of(beyond, reach, root), beyond[3 * scen :])
 
     s, u = [start], [precondition(start)]
     for j in range(ITERS):
         v = u[j]
-        halo_out[j, 0] = v[:, :LANES]
-        halo_out[j, 1] = v[:, LANES:]
-        copies = exchange(halo_out.at[j], halo_in.at[j], halo_send.at[j], halo_recv.at[j])
+        copies = []
+        if j:
+            halo_out[j - 1, 0] = v[:, :LANES]
+            halo_out[j - 1, 1] = v[:, LANES:]
+            copies = exchange(
+                halo_out.at[j - 1], halo_in.at[j - 1], halo_send.at[j - 1], halo_recv.at[j - 1]
+            )
         ends = select_dot(v, gather_tab[...], 2)
         f0, f1, t0, t1 = ends[:scen, :span], ends[scen:, :span], ends[:scen, span:], ends[scen:, span:]
         terms = jnp.concatenate(
@@ -316,9 +346,11 @@
         )
         inside_sum = select_dot(terms, scatter_tab[...], 2)
         for copy in copies:
-            copy.wait()
-        n0 = jnp.concatenate([halo_in[j, 0, :scen], halo_in[j, 1, :scen]], axis=1)
-        n1 = jnp.concatenate([halo_in[j, 0, scen:], halo_in[j, 1, scen:]], axis=1)
+            copy.wait_recv()
+        pending.extend(copies)
+        if j:
+            facing = jnp.concatenate([halo_in[j - 1, 0], halo_in[j - 1, 1]], axis=1)
+        n0, n1 = facing[:scen], facing[scen:]
         s.append(inside_sum + jnp.concatenate([c00 * n0 + c01 * n1, c10 * n0 + c11 * n1], axis=0))
         if j + 1 < ITERS:
             u.append(precondition(s[-1]))
@@ -338,7 +370,8 @@
             copy.start()
             copies.append(copy)
         for copy in copies:
-            copy.wait()
+            copy.wait_recv()
+        pending.extend(copies)
         total = red_a[0]
         for k in range(1, group):
             total = total + red_a[k]
@@ -356,27 +389,29 @@
             copy.start()
             copies.append(copy)
         for copy in copies:
-            copy.wait()
+            copy.wait_recv()
+        pending.extend(copies)
         total = red_b[0]
         for k in range(1, outer):
             total = total + red_b[k]
         return total
 
-    total = all_sum(pack([inner(u[k // 2], s[k - k // 2]) for k in range(2 * ITERS)]))
-    moments = [total] + [pltpu.roll(total, LANES - 4 * m, 1) for m in range(1, 2 * ITERS)]
+    parts = [inner(u[k // 2], s[k - k // 2]) for k in range(2 * ITERS)]
+    total = all_sum(jnp.concatenate([pack(parts[:4]), pack(parts[4:])], axis=0))
+    moments = [total[k // 4 : k // 4 + 1] for k in range(2 * ITERS)]
+    moments = [pltpu.roll(m, LANES - 32 * (k % 4), 1) if k % 4 else m for k, m in enumerate(moments)]
     gram = {(i, j): moments[i + j] + moments[i + j + 1] for i in range(ITERS) for j in range(i, ITERS)}
-    weights = galerkin(gram, moments[:ITERS], ITERS)
-    weights = [unpack(w) for w in weights]
-    weights = [jnp.concatenate([w, w], axis=0) for w in weights]
-    step = weights[0] * u[0]
-    residual = s[0] - weights[0] * (s[0] + s[1])
-    for j in range(1, ITERS):
-        step = step + weights[j] * u[j]
-        residual = residual - weights[j] * (s[j] + s[j + 1])
+    w = unpack(galerkin(gram, moments[ITERS:], ITERS))
+    w = [jnp.concatenate([jnp.concatenate([c, c], axis=1)] * 2, axis=0) for c in w]
+    step = (1.0 + w[0]) * u[0] + (w[1] - 1.0) * u[1] + (1.0 + w[2]) * u[2] + (w[3] - 1.0) * u[3]
+    residual = (1.0 - w[3]) * s[4] - (w[2] + w[3]) * s[3] - (w[1] + w[2]) * s[2] - (w[0] + w[1]) * s[1] - w[0] * s[0]
     out = select_dot(jnp.concatenate([step, residual], axis=0), to_bus, 3)
     for c in range(2):
         x_ref[c] = out[c * scen : (c + 1) * scen, :buses]
         r_ref[c] = out[(2 + c) * scen : (3 + c) * scen, :buses]
+
+    for copy in pending:
+        copy.wait_send()
 
 
 def body(
@@ -418,11 +453,11 @@
         row(gen_bus),
         row(gen_curvature),
     )
-    step, residual = pl.pallas_call(
+    both = pl.pallas_call(
         functools.partial(kernel, n, group),
-        out_shape=[jax.ShapeDtypeStruct((2, scen, buses), F32)] * 2,
+        out_shape=pltpu.VMEM((2, 2, scen, buses), F32),
         in_specs=[pl.BlockSpec(memory_space=pltpu.HBM)] * 13,
-        out_specs=[pl.BlockSpec(memory_space=pltpu.VMEM)] * 2,
+        out_specs=pl.BlockSpec(memory_space=pltpu.VMEM),
         scratch_shapes=[
             *(pltpu.VMEM(a.shape, a.dtype) for a in operands),
             dma(13),
@@ -433,14 +468,18 @@
             pltpu.VMEM((2 * span, 2 * LANES), BF16),
             pltpu.VMEM((2, rows, LANES), F32),
             pltpu.VMEM((2, rows, LANES), F32),
-            pltpu.VMEM((ITERS, 2, 2 * scen, LANES), F32),
-            pltpu.VMEM((ITERS, 2, 2 * scen, LANES), F32),
-            pltpu.VMEM((group, 8, LANES), F32),
-            pltpu.VMEM((outer, 8, LANES), F32),
+            pltpu.VMEM((2, 5 * scen, LANES), F32),
+            pltpu.VMEM((2, 5 * scen, LANES), F32),
+            pltpu.VMEM((ITERS - 1, 2, 2 * scen, LANES), F32),
+            pltpu.VMEM((ITERS - 1, 2, 2 * scen, LANES), F32),
+            pltpu.VMEM((group, 2, LANES), F32),
+            pltpu.VMEM((outer, 2, LANES), F32),
             dma(2),
             dma(2),
-            dma(ITERS, 2),
-            dma(ITERS, 2),
+            dma(2),
+            dma(2),
+            dma(ITERS - 1, 2),
+            dma(ITERS - 1, 2),
             dma(group),
             dma(group),
             dma(outer),
@@ -451,7 +490,7 @@
         ),
         name="newton",
     )(*operands)
-    return step.transpose(2, 0, 1), residual.transpose(2, 0, 1)
+    return both[0].transpose(2, 0, 1), both[1].transpose(2, 0, 1)
 
 
 def solution(mesh):

time: 46.6 us -> 41.2 us (0.88)
  Pallas kernels: 43 us -> 39 us
  local copies, waits for them, and re-layouts: 2.14 us -> 0.66 us
    pallas_call x1, Pallas kernels: 43 us -> 39 us  [body(): pl.pallas_call(functools.partial(kernel, n, group), out_shape=pltpu.VMEM(...]
    unnamed x4 -> x0, local copies, waits for them, and re-layouts: 2.14 us -> none
    transpose x0 -> x1, local copies, waits for them, and re-layouts: none -> 0.66 us  [body(): return (both[0].transpose(2, 0, 1), both[1].transpose(2, 0, 1))]
where the time goes in v3:
time: 41.2 us; the launch traced here: 40.9 us
  Pallas kernels  39 us (95%)
  between operations  1.29 us (3%)
  local copies, waits for them, and re-layouts  0.66 us (2%)
    pallas_call x1, Pallas kernels, body(): pl.pallas_call(functools.partial(kernel, n, group), out_shape=pltpu.VMEM(...  39 us

profile of v3, /device:TPU:1, one launch (start us, length us, event | category | flops | bytes accessed | tf_op | source)
XLA Modules:
  0.0 40.9 jit_solution(17141298150593359563)
XLA Ops:
  1.3 39.0 %newton.1 = f32[2,2,32,240]{3,2,1,0:T(8,128)S(1)} custom-call(f32[32,240]{1,0:T(8,128)} %bitcast.19, f32[32,240]{1,0:T(8,128)} %bitcast.20, f32[2,32,240]{2,1,0:T(8,128)} %bitcast.18, s32[320]{0:T(512)} %refs_3_.1, s32[320]{0:T(512)} %refs_4_.1, s32[1]{0:T(128)S(6)} %copy.15.refs_5_, s32[1,240]{1,0:T(1,128)} %bitcast.21, f32[320]{0:T(512)} %refs_7_.1, ...), custom_call_target="tpu_custom_call" | custom-call | tf_op jit(solution)/shard_map/newton/pallas_call | solution.py:456
  40.3 0.7 %slice_bitcast_fusion = (f32[240,2,32]{0,2,1:T(8,128)}, f32[240,2,32]{0,2,1:T(8,128)}) fusion(f32[2,2,32,240]{3,2,1,0:T(8,128)S(1)} %newton.1), kind=kLoop, calls=%fused_computation | loop fusion | bytes 245760 | tf_op jit(solution)/shard_map/transpose | solution.py:493

commit v4 on v3

--- a/solution.py
+++ b/solution.py
@@ -11,6 +11,7 @@
 F32, BF16 = jnp.float32, jnp.bfloat16
 ITERS = 4
 LANES = 128
+OWN = 2
 
 barrier_weight = 0.01
 volt_low = 0.9
@@ -117,7 +118,7 @@
     x_ref, r_ref = o_ref.at[0], o_ref.at[1]
     load_sem = rest[0]
     me = lax.axis_index("net")
-    neighbours = (lax.rem(me + n - 1, n), lax.rem(me + 1, n))
+    neighbours = [lax.rem(me + n + d, n) for d in (-1, 1, -2, 2)]
     for peer in neighbours:
         pl.semaphore_signal(pltpu.get_barrier_semaphore(), inc=1, device_id={"net": peer}, device_id_type=MESH)
     loads = []
@@ -152,20 +153,21 @@
     vin,
     gather_tab,
     scatter_tab,
-    pay_out,
-    pay_in,
-    diag_out,
-    diag_in,
-    halo_out,
-    halo_in,
+    blocks,
+    a_out,
+    a_in,
+    f_in,
+    b_out,
+    b_in,
+    w_out,
+    w_in,
+    x_out,
+    x_in,
+    y_in,
     red_a,
     red_b,
-    pay_send,
-    pay_recv,
-    diag_send,
-    diag_recv,
-    halo_send,
-    halo_recv,
+    send_sem,
+    recv_sem,
     a_send,
     a_recv,
     b_send,
@@ -175,34 +177,34 @@
     slots = from_ref.shape[-1]
     ghost = buses // 2
     wide = 2 * LANES
-    span = gather_tab.shape[1] // 2
+    span = gather_tab.shape[2] // 2
     gens = gbus_ref.shape[1]
     outer = n // group
     me = lax.axis_index("net")
-    prev, nxt = lax.rem(me + n - 1, n), lax.rem(me + 1, n)
-    inside = lax.rem(me, group)
+    prev, nxt, prev2, nxt2 = [lax.rem(me + n + d, n) for d in (-1, 1, -2, 2)]
+    member = lax.rem(me, group)
     block = lax.div(me, group)
-    peers_a = [block * group + lax.rem(inside + d, group) for d in range(1, group)]
-    peers_b = [lax.rem(block + d, outer) * group + inside for d in range(1, outer)]
+    peers_a = [block * group + lax.rem(member + d, group) for d in range(1, group)]
+    peers_b = [lax.rem(block + d, outer) * group + member for d in range(1, outer)]
 
     barrier = pltpu.get_barrier_semaphore()
     for peer in (*peers_a, *peers_b):
         pl.semaphore_signal(barrier, inc=1, device_id={"net": peer}, device_id_type=MESH)
 
-    def exchange(source, target, send, recv):
-        out = []
-        for half, peer in ((0, prev), (1, nxt)):
-            copy = pltpu.make_async_remote_copy(
-                src_ref=source.at[half],
-                dst_ref=target.at[1 - half],
-                send_sem=send.at[half],
-                recv_sem=recv.at[half],
-                device_id={"net": peer},
-                device_id_type=MESH,
-            )
-            copy.start()
-            out.append(copy)
-        return out
+    pending = []
+
+    def send(message, source, target, peer):
+        copy = pltpu.make_async_remote_copy(
+            src_ref=source,
+            dst_ref=target,
+            send_sem=send_sem.at[message],
+            recv_sem=recv_sem.at[message],
+            device_id={"net": peer},
+            device_id_type=MESH,
+        )
+        copy.start()
+        pending.append(copy)
+        return copy
 
     for copy in loads:
         copy.wait()
@@ -231,15 +233,21 @@
     def hot(mask):
         return jnp.where(mask, 1.0, 0.0).astype(BF16)
 
-    place_col, from_col, to_col = column(place), column(from_row), column(to_row)
     lanes_of = lambda row, t: row[:, t * LANES : (t + 1) * LANES]
-    for t in range(span // LANES):
-        gather_tab[:, t * LANES : (t + 1) * LANES] = hot(place_col == lanes_of(from_row, t))
-        gather_tab[:, span + t * LANES : span + (t + 1) * LANES] = hot(place_col == lanes_of(to_row, t))
-    for t in range(2):
-        cols = slice(t * LANES, (t + 1) * LANES)
-        scatter_tab[0:span, cols] = hot(from_col == lanes_of(place, t))
-        scatter_tab[span:, cols] = hot(to_col == lanes_of(place, t))
+
+    def index_tables(k, place, from_row, to_row):
+        place_col, from_col, to_col = column(place), column(from_row), column(to_row)
+        for t in range(span // LANES):
+            gather_tab[k, :, t * LANES : (t + 1) * LANES] = hot(place_col == lanes_of(from_row, t))
+            gather_tab[k, :, span + t * LANES : span + (t + 1) * LANES] = hot(place_col == lanes_of(to_row, t))
+        for t in range(2):
+            cols = slice(t * LANES, (t + 1) * LANES)
+            scatter_tab[k, 0:span, cols] = hot(from_col == lanes_of(place, t))
+            scatter_tab[k, span:, cols] = hot(to_col == lanes_of(place, t))
+        return place_col, to_col
+
+    place_col, to_col = index_tables(OWN, place, from_row, to_row)
+    irow[4:5, :wide] = place
     cross_tab = jnp.concatenate([hot(to_col == lanes_of(entry, t) + buses) for t in range(2)], axis=1)
     bus_row = lane[0:1]
     bus_col = lax.broadcasted_iota(jnp.int32, (wide, LANES), 0).astype(F32)
@@ -263,105 +271,159 @@
     stacked = jnp.concatenate([weight_p, weight_q, frow[0:8, :]], axis=0)
     crossing = select_dot(stacked, cross_tab, 3)
     payload = jnp.concatenate([vm, va, crossing], axis=0)
-    for half in range(2):
-        pay_out[half] = payload[:, half * LANES : (half + 1) * LANES]
-
-    pl.semaphore_wait(barrier, 2 + (group - 1) + (outer - 1))
-    pay_copies = exchange(pay_out, pay_in, pay_send, pay_recv)
-
-    ends = select_dot(placed[0 : 2 * scen], gather_tab[...], 3)
+    split = lambda v: (v[:, :LANES], v[:, LANES:])
+    join = lambda a, b: jnp.concatenate([a, b], axis=1)
+    for half, part in enumerate(split(payload)):
+        a_out[half] = part
+
+    pl.semaphore_wait(barrier, 4 + (group - 1) + (outer - 1))
+    a_near = [send(0, a_out.at[0], a_in.at[1, 0], prev), send(1, a_out.at[1], a_in.at[0, 1], nxt)]
+
+    def local_blocks(k, volts, weight_p, weight_q, conduct, suscept):
+        ends = select_dot(volts, gather_tab[k], 3)
+        sine, cosine = sine_cosine(ends[scen:, :span] - ends[scen:, span:])
+        hff, htt, hft = branch_blocks(
+            ends[:scen, :span], ends[:scen, span:], sine, cosine, conduct, suscept, weight_p, weight_q
+        )
+        for e in range(4):
+            blocks[k, e] = hft[e]
+        return hff, htt
+
     local = jnp.where((to_row >= 0.0) & (to_row < float(buses)), 1.0, 0.0)
-    sine, cosine = sine_cosine(ends[scen:, :span] - ends[scen:, span:])
-    hff, htt, (h00, h01, h10, h11) = branch_blocks(
-        ends[:scen, :span], ends[:scen, span:], sine, cosine, conduct, suscept, weight_p * local, weight_q * local
-    )
-    both = jnp.concatenate([jnp.concatenate([a, b], axis=1) for a, b in zip(hff, htt)], axis=0)
-    diag = select_dot(both, scatter_tab[...], 3)
+    weight_p, weight_q = weight_p * local, weight_q * local
+    hff, htt = local_blocks(OWN, placed[0 : 2 * scen], weight_p, weight_q, conduct, suscept)
+    both = jnp.concatenate([join(a, b) for a, b in zip(hff, htt)], axis=0)
+    diag = select_dot(both, scatter_tab[OWN], 3)
     gen = column(irow[3:4, :LANES])
     curve = column(frow[2:3, :LANES])
-    gen_sum = jnp.concatenate(
-        [jnp.sum(jnp.where(gen == lanes_of(place, t), curve, 0.0), axis=0, keepdims=True) for t in range(2)], axis=1
+    gen_sum = join(
+        *(jnp.sum(jnp.where(gen == lanes_of(place, t), curve, 0.0), axis=0, keepdims=True) for t in range(2))
     )
     low, high = vm - volt_low, volt_high - vm
     base_vv = barrier_weight / (low * low) + barrier_weight / (high * high) + gen_sum
     base_aa = angle_reg + gen_sum
-
     own = jnp.concatenate(
         [diag[0:scen] + base_vv, diag[scen : 2 * scen], diag[2 * scen :] + base_aa, start], axis=0
     )
-    for half in range(2):
-        diag_out[half] = own[:, half * LANES : (half + 1) * LANES]
-    diag_copies = exchange(diag_out, diag_in, diag_send, diag_recv)
-    pending = [*pay_copies, *diag_copies]
-
-    for copy in pay_copies:
-        copy.wait_recv()
-    arrived = jnp.concatenate([pay_in[0], pay_in[1]], axis=1)
-    there_vm, there_va = arrived[0:scen], arrived[scen : 2 * scen]
-    there_p, there_q = arrived[2 * scen : 3 * scen], arrived[3 * scen : 4 * scen]
-    there_g, there_b = arrived[4 * scen : 4 * scen + 1], arrived[4 * scen + 1 : 4 * scen + 2]
-    here_p, here_q = crossing[0:scen], crossing[scen : 2 * scen]
-    here_g, here_b = crossing[2 * scen : 2 * scen + 1], crossing[2 * scen + 1 : 2 * scen + 2]
-    sine, cosine = sine_cosine(va - there_va)
-    off, reach, (o00, o01, o10, o11) = branch_blocks(vm, there_vm, sine, cosine, here_g, here_b, here_p, here_q)
-    root, on, (i00, i01, i10, i11) = branch_blocks(there_vm, vm, -sine, cosine, there_g, there_b, there_p, there_q)
-    c00, c01, c10, c11 = o00 + i00, o01 + i10, o10 + i01, o11 + i11
-
-    def inverse_of(fields, first, second):
+    for half, part in enumerate(split(own)):
+        b_out[half] = part
+    b_near = [send(2, b_out.at[0], b_in.at[1, 0], prev), send(3, b_out.at[1], b_in.at[0, 1], nxt)]
+
+    w_out[0:scen] = weight_p
+    w_out[scen : 2 * scen] = weight_q
+    w_out[2 * scen : 2 * scen + 8] = irow[...]
+    w_out[2 * scen + 8 :] = frow[...]
+    rows = pl.ds(0, 3 * scen)
+    far = [
+        send(4, w_out, w_in.at[1], prev),
+        send(5, w_out, w_in.at[0], nxt),
+        send(6, a_out.at[1], a_in.at[1, 1], prev),
+        send(7, a_out.at[0], a_in.at[0, 0], nxt),
+        send(8, a_out.at[0], f_in.at[1], prev2),
+        send(9, a_out.at[1], f_in.at[0], nxt2),
+        send(10, b_out.at[1, rows], b_in.at[1, 1, rows], prev),
+        send(11, b_out.at[0, rows], b_in.at[0, 0, rows], nxt),
+    ]
+
+    def coupling(here, there):
+        vm, va, p, q = (here[k * scen : (k + 1) * scen] for k in range(4))
+        there_vm, there_va, there_p, there_q = (there[k * scen : (k + 1) * scen] for k in range(4))
+        g, b = here[4 * scen : 4 * scen + 1], here[4 * scen + 1 : 4 * scen + 2]
+        there_g, there_b = there[4 * scen : 4 * scen + 1], there[4 * scen + 1 : 4 * scen + 2]
+        sine, cosine = sine_cosine(va - there_va)
+        off, reach, (o00, o01, o10, o11) = branch_blocks(vm, there_vm, sine, cosine, g, b, p, q)
+        root, on, (i00, i01, i10, i11) = branch_blocks(there_vm, vm, -sine, cosine, there_g, there_b, there_p, there_q)
+        return (off, on), (reach, root), (o00 + i00, o01 + i10, o10 + i01, o11 + i11)
+
+    def inverse_of(fields, parts):
+        first, second = parts
         d00, d01, d11 = (fields[k * scen : (k + 1) * scen] + first[k] + second[k] for k in range(3))
         inverse = 1.0 / (d00 * d11 - d01 * d01)
         return d11 * inverse, -d01 * inverse, d00 * inverse
 
-    def applied(blocks, v):
-        b00, b01, b11 = blocks
+    def applied(fields, v):
+        b00, b01, b11 = fields
         return jnp.concatenate([b00 * v[:scen] + b01 * v[scen:], b01 * v[:scen] + b11 * v[scen:]], axis=0)
 
-    diag_inverse = inverse_of(own, off, on)
-    def precondition(v):
-        return applied(diag_inverse, v)
-
-    for copy in diag_copies:
+    def coupled(c, v):
+        v0, v1 = v[:scen], v[scen:]
+        return jnp.concatenate([c[0] * v0 + c[1] * v1, c[2] * v0 + c[3] * v1], axis=0)
+
+    for copy in a_near:
         copy.wait_recv()
-    beyond = jnp.concatenate([diag_in[0], diag_in[1]], axis=1)
-    facing = applied(inverse_of(beyond, reach, root), beyond[3 * scen :])
-
-    s, u = [start], [precondition(start)]
-    for j in range(ITERS):
-        v = u[j]
-        copies = []
-        if j:
-            halo_out[j - 1, 0] = v[:, :LANES]
-            halo_out[j - 1, 1] = v[:, LANES:]
-            copies = exchange(
-                halo_out.at[j - 1], halo_in.at[j - 1], halo_send.at[j - 1], halo_recv.at[j - 1]
-            )
-        ends = select_dot(v, gather_tab[...], 2)
+    here_parts, there_parts, border = coupling(payload, join(a_in[0, 1], a_in[1, 0]))
+    border_back = (border[0], border[2], border[1], border[3])
+    diag_inverse = inverse_of(own, here_parts)
+
+    for copy in b_near:
+        copy.wait_recv()
+    beyond = join(b_in[0, 1], b_in[1, 0])
+    facing_inverse = inverse_of(beyond, there_parts)
+    facing = applied(facing_inverse, beyond[3 * scen :])
+
+    def inside_product(k, v):
+        ends = select_dot(v, gather_tab[k], 2)
         f0, f1, t0, t1 = ends[:scen, :span], ends[scen:, :span], ends[:scen, span:], ends[scen:, span:]
+        h00, h01, h10, h11 = (blocks[k, e] for e in range(4))
         terms = jnp.concatenate(
             [
-                jnp.concatenate([h00 * t0 + h01 * t1, h00 * f0 + h10 * f1], axis=1),
-                jnp.concatenate([h10 * t0 + h11 * t1, h01 * f0 + h11 * f1], axis=1),
+                join(h00 * t0 + h01 * t1, h00 * f0 + h10 * f1),
+                join(h10 * t0 + h11 * t1, h01 * f0 + h11 * f1),
             ],
             axis=0,
         )
-        inside_sum = select_dot(terms, scatter_tab[...], 2)
-        for copy in copies:
-            copy.wait_recv()
-        pending.extend(copies)
-        if j:
-            facing = jnp.concatenate([halo_in[j - 1, 0], halo_in[j - 1, 1]], axis=1)
-        n0, n1 = facing[:scen], facing[scen:]
-        s.append(inside_sum + jnp.concatenate([c00 * n0 + c01 * n1, c10 * n0 + c11 * n1], axis=0))
-        if j + 1 < ITERS:
-            u.append(precondition(s[-1]))
+        return select_dot(terms, scatter_tab[k], 2)
+
+    s, u = [start], [applied(diag_inverse, start)]
+    s.append(inside_product(OWN, u[0]) + coupled(border, facing))
+    u.append(applied(diag_inverse, s[1]))
+    for half, part in enumerate(split(u[1])):
+        x_out[half] = part
+    vectors = [
+        send(12, x_out, x_in.at[1], prev),
+        send(13, x_out, x_in.at[0], nxt),
+        send(14, x_out.at[0], y_in.at[1], prev2),
+        send(15, x_out.at[1], y_in.at[0], nxt2),
+    ]
+
+    for copy in far:
+        copy.wait_recv()
+    inside = inside_product(OWN, u[1])
+    outer_border, side_inverse = [], []
+    for k in range(2):
+        index, value = w_in[k, 2 * scen : 2 * scen + 8], w_in[k, 2 * scen + 8 :]
+        index_tables(k, index[4:5, :wide], index[0:1], index[1:2])
+        volts = join(a_in[k, 0, : 2 * scen], a_in[k, 1, : 2 * scen])
+        local_blocks(k, volts, w_in[k, :scen], w_in[k, scen : 2 * scen], value[0:1], value[1:2])
+        parts, _, fields = coupling(a_in[k, k], f_in[k])
+        outer_border.append(fields)
+        outside = inverse_of(b_in[k, k, : 3 * scen], parts)
+        near = [split(f)[k] for f in facing_inverse]
+        side_inverse.append([join(f, g) if k else join(g, f) for f, g in zip(near, outside)])
+
+    for copy in vectors:
+        copy.wait_recv()
+    side = [join(x_in[k, 0], x_in[k, 1]) for k in range(2)]
+    for j in (2, 3):
+        facing = join(split(side[0])[1], split(side[1])[0])
+        s.append(inside + coupled(border, facing))
+        back = split(coupled(border_back, u[-1]))
+        for k in range(2):
+            near, outside = back[k], coupled(outer_border[k], y_in[k]) if j == 2 else jnp.zeros_like(back[k])
+            product = inside_product(k, side[k]) + (join(near, outside) if k else join(outside, near))
+            side[k] = applied(side_inverse[k], product)
+        u.append(applied(diag_inverse, s[-1]))
+        inside = inside_product(OWN, u[-1])
+    facing = join(split(side[0])[1], split(side[1])[0])
+    s.append(inside + coupled(border, facing))
 
     def all_sum(tile):
-        red_a[pl.ds(inside, 1)] = tile[None]
+        red_a[pl.ds(member, 1)] = tile[None]
         copies = []
         for d, peer in enumerate(peers_a):
             copy = pltpu.make_async_remote_copy(
-                src_ref=red_a.at[inside],
-                dst_ref=red_a.at[inside],
+                src_ref=red_a.at[member],
+                dst_ref=red_a.at[member],
                 send_sem=a_send.at[d],
                 recv_sem=a_recv.at[d],
                 device_id={"net": peer},
@@ -464,22 +526,23 @@
             pltpu.VMEM((8, span), F32),
             pltpu.VMEM((8, span), F32),
             pltpu.VMEM((4 * scen, 2 * LANES), F32),
-            pltpu.VMEM((2 * LANES, 2 * span), BF16),
-            pltpu.VMEM((2 * span, 2 * LANES), BF16),
+            pltpu.VMEM((3, 2 * LANES, 2 * span), BF16),
+            pltpu.VMEM((3, 2 * span, 2 * LANES), BF16),
+            pltpu.VMEM((3, 4, scen, span), F32),
             pltpu.VMEM((2, rows, LANES), F32),
+            pltpu.VMEM((2, 2, rows, LANES), F32),
             pltpu.VMEM((2, rows, LANES), F32),
             pltpu.VMEM((2, 5 * scen, LANES), F32),
-            pltpu.VMEM((2, 5 * scen, LANES), F32),
-            pltpu.VMEM((ITERS - 1, 2, 2 * scen, LANES), F32),
-            pltpu.VMEM((ITERS - 1, 2, 2 * scen, LANES), F32),
+            pltpu.VMEM((2, 2, 5 * scen, LANES), F32),
+            pltpu.VMEM((2 * scen + 16, span), F32),
+            pltpu.VMEM((2, 2 * scen + 16, span), F32),
+            pltpu.VMEM((2, 2 * scen, LANES), F32),
+            pltpu.VMEM((2, 2, 2 * scen, LANES), F32),
+            pltpu.VMEM((2, 2 * scen, LANES), F32),
             pltpu.VMEM((group, 2, LANES), F32),
             pltpu.VMEM((outer, 2, LANES), F32),
-            dma(2),
-            dma(2),
-            dma(2),
-            dma(2),
-            dma(ITERS - 1, 2),
-            dma(ITERS - 1, 2),
+            dma(16),
+            dma(16),
             dma(group),
             dma(group),
             dma(outer),

time: 41.2 us -> 37.2 us (0.903)
  Pallas kernels: 39 us -> 35.1 us
    pallas_call x1, Pallas kernels: 39 us -> 35.1 us  [body(): pl.pallas_call(functools.partial(kernel, n, group), out_shape=pltpu.VMEM(...]
where the time goes in v4:
time: 37.2 us; the launch traced here: 37 us
  Pallas kernels  35.1 us (94%)
  between operations  1.29 us (3%)
  local copies, waits for them, and re-layouts  0.66 us (2%)
    pallas_call x1, Pallas kernels, body(): pl.pallas_call(functools.partial(kernel, n, group), out_shape=pltpu.VMEM(...  35.1 us

profile of v4, /device:TPU:1, one launch (start us, length us, event | category | flops | bytes accessed | tf_op | source)
XLA Modules:
  0.0 37.0 jit_solution(5079497021178796577)
XLA Ops:
  1.3 35.1 %newton.1 = f32[2,2,32,240]{3,2,1,0:T(8,128)S(1)} custom-call(f32[32,240]{1,0:T(8,128)} %bitcast.19, f32[32,240]{1,0:T(8,128)} %bitcast.20, f32[2,32,240]{2,1,0:T(8,128)} %bitcast.18, s32[320]{0:T(512)} %refs_3_.1, s32[320]{0:T(512)} %refs_4_.1, s32[1]{0:T(128)S(6)} %copy.15.refs_5_, s32[1,240]{1,0:T(1,128)} %bitcast.21, f32[320]{0:T(512)} %refs_7_.1, ...), custom_call_target="tpu_custom_call" | custom-call | tf_op jit(solution)/shard_map/newton/pallas_call | solution.py:518
  36.4 0.7 %slice_bitcast_fusion = (f32[240,2,32]{0,2,1:T(8,128)}, f32[240,2,32]{0,2,1:T(8,128)}) fusion(f32[2,2,32,240]{3,2,1,0:T(8,128)S(1)} %newton.1), kind=kLoop, calls=%fused_computation | loop fusion | bytes 245760 | tf_op jit(solution)/shard_map/transpose | solution.py:556

commit v5 on v4

--- a/solution.py
+++ b/solution.py
@@ -109,6 +109,10 @@
     return out
 
 
+def partners(n):
+    return (-1, 1, -2, 2, -16, 16) if n > 32 else (-1, 1, -2, 2)
+
+
 def kernel(
     n,
     group,
@@ -118,7 +122,7 @@
     x_ref, r_ref = o_ref.at[0], o_ref.at[1]
     load_sem = rest[0]
     me = lax.axis_index("net")
-    neighbours = [lax.rem(me + n + d, n) for d in (-1, 1, -2, 2)]
+    neighbours = [lax.rem(me + n + d, n) for d in partners(n)]
     for peer in neighbours:
         pl.semaphore_signal(pltpu.get_barrier_semaphore(), inc=1, device_id={"net": peer}, device_id_type=MESH)
     loads = []
@@ -172,6 +176,7 @@
     a_recv,
     b_send,
     b_recv,
+    known_sem,
 ):
     scen, buses = vm_ref.shape
     slots = from_ref.shape[-1]
@@ -188,9 +193,22 @@
     peers_b = [lax.rem(block + d, outer) * group + member for d in range(1, outer)]
 
     barrier = pltpu.get_barrier_semaphore()
-    for peer in (*peers_a, *peers_b):
-        pl.semaphore_signal(barrier, inc=1, device_id={"net": peer}, device_id_type=MESH)
-
+    spans = [[d for d in step if d < n // 2] for step in ((2, 16), (4, 32), (8,))]
+
+    def tell(step):
+        for d in spans[step]:
+            for at in (n - d, d):
+                pl.semaphore_signal(
+                    known_sem.at[step], inc=1, device_id={"net": lax.rem(me + at, n)}, device_id_type=MESH
+                )
+
+    def told(step):
+        if spans[step]:
+            pl.semaphore_wait(known_sem.at[step], 2 * len(spans[step]))
+
+    core = lax.rem(me, 2)
+    mate = me + 1 - 2 * core
+    beyond_mate = lax.rem(me + n + 2 - 4 * core, n)
     pending = []
 
     def send(message, source, target, peer):
@@ -276,7 +294,7 @@
     for half, part in enumerate(split(payload)):
         a_out[half] = part
 
-    pl.semaphore_wait(barrier, 4 + (group - 1) + (outer - 1))
+    pl.semaphore_wait(barrier, len(partners(n)))
     a_near = [send(0, a_out.at[0], a_in.at[1, 0], prev), send(1, a_out.at[1], a_in.at[0, 1], nxt)]
 
     def local_blocks(k, volts, weight_p, weight_q, conduct, suscept):
@@ -309,18 +327,19 @@
         b_out[half] = part
     b_near = [send(2, b_out.at[0], b_in.at[1, 0], prev), send(3, b_out.at[1], b_in.at[0, 1], nxt)]
 
+    tell(0)
+
     w_out[0:scen] = weight_p
     w_out[scen : 2 * scen] = weight_q
-    w_out[2 * scen : 2 * scen + 8] = irow[...]
-    w_out[2 * scen + 8 :] = frow[...]
+    irow[5:7] = frow[0:2]
+    w_out[2 * scen :] = irow[...]
     rows = pl.ds(0, 3 * scen)
     far = [
         send(4, w_out, w_in.at[1], prev),
         send(5, w_out, w_in.at[0], nxt),
         send(6, a_out.at[1], a_in.at[1, 1], prev),
         send(7, a_out.at[0], a_in.at[0, 0], nxt),
-        send(8, a_out.at[0], f_in.at[1], prev2),
-        send(9, a_out.at[1], f_in.at[0], nxt2),
+        send(8, a_out.at[1 - core], f_in.at[core], beyond_mate),
         send(10, b_out.at[1, rows], b_in.at[1, 1, rows], prev),
         send(11, b_out.at[0, rows], b_in.at[0, 0, rows], nxt),
     ]
@@ -351,6 +370,9 @@
 
     for copy in a_near:
         copy.wait_recv()
+    told(0)
+    tell(1)
+    far.append(send(9, a_in.at[core, 1 - core], f_in.at[core], mate))
     here_parts, there_parts, border = coupling(payload, join(a_in[0, 1], a_in[1, 0]))
     border_back = (border[0], border[2], border[1], border[3])
     diag_inverse = inverse_of(own, here_parts)
@@ -386,15 +408,18 @@
         send(15, x_out.at[1], y_in.at[0], nxt2),
     ]
 
+    told(1)
+    tell(2)
+
     for copy in far:
         copy.wait_recv()
     inside = inside_product(OWN, u[1])
     outer_border, side_inverse = [], []
     for k in range(2):
-        index, value = w_in[k, 2 * scen : 2 * scen + 8], w_in[k, 2 * scen + 8 :]
+        index = w_in[k, 2 * scen :]
         index_tables(k, index[4:5, :wide], index[0:1], index[1:2])
         volts = join(a_in[k, 0, : 2 * scen], a_in[k, 1, : 2 * scen])
-        local_blocks(k, volts, w_in[k, :scen], w_in[k, scen : 2 * scen], value[0:1], value[1:2])
+        local_blocks(k, volts, w_in[k, :scen], w_in[k, scen : 2 * scen], index[5:6], index[6:7])
         parts, _, fields = coupling(a_in[k, k], f_in[k])
         outer_border.append(fields)
         outside = inverse_of(b_in[k, k, : 3 * scen], parts)
@@ -458,6 +483,7 @@
             total = total + red_b[k]
         return total
 
+    told(2)
     parts = [inner(u[k // 2], s[k - k // 2]) for k in range(2 * ITERS)]
     total = all_sum(jnp.concatenate([pack(parts[:4]), pack(parts[4:])], axis=0))
     moments = [total[k // 4 : k // 4 + 1] for k in range(2 * ITERS)]
@@ -534,8 +560,8 @@
             pltpu.VMEM((2, rows, LANES), F32),
             pltpu.VMEM((2, 5 * scen, LANES), F32),
             pltpu.VMEM((2, 2, 5 * scen, LANES), F32),
-            pltpu.VMEM((2 * scen + 16, span), F32),
-            pltpu.VMEM((2, 2 * scen + 16, span), F32),
+            pltpu.VMEM((2 * scen + 8, span), F32),
+            pltpu.VMEM((2, 2 * scen + 8, span), F32),
             pltpu.VMEM((2, 2 * scen, LANES), F32),
             pltpu.VMEM((2, 2, 2 * scen, LANES), F32),
             pltpu.VMEM((2, 2 * scen, LANES), F32),
@@ -547,6 +573,7 @@
             dma(group),
             dma(outer),
             dma(outer),
+            pltpu.SemaphoreType.REGULAR((3,)),
         ],
         compiler_params=pltpu.CompilerParams(
             collective_id=0, has_side_effects=True, vmem_limit_bytes=62 * 1024 * 1024

time: 37.2 us -> 35.2 us (0.946)
  Pallas kernels: 35.1 us -> 33.1 us
    pallas_call x1, Pallas kernels: 35.1 us -> 33.1 us  [body(): pl.pallas_call(functools.partial(kernel, n, group), out_shape=pltpu.VMEM(...]
where the time goes in v5:
time: 35.2 us; the launch traced here: 35.1 us
  Pallas kernels  33.1 us (94%)
  between operations  1.29 us (4%)
  local copies, waits for them, and re-layouts  0.66 us (2%)
    pallas_call x1, Pallas kernels, body(): pl.pallas_call(functools.partial(kernel, n, group), out_shape=pltpu.VMEM(...  33.1 us

profile of v5, /device:TPU:1, one launch (start us, length us, event | category | flops | bytes accessed | tf_op | source)
XLA Modules:
  0.0 35.1 jit_solution(9991478407630766946)
XLA Ops:
  1.3 33.1 %newton.1 = f32[2,2,32,240]{3,2,1,0:T(8,128)S(1)} custom-call(f32[32,240]{1,0:T(8,128)} %bitcast.19, f32[32,240]{1,0:T(8,128)} %bitcast.20, f32[2,32,240]{2,1,0:T(8,128)} %bitcast.18, s32[320]{0:T(512)} %refs_3_.1, s32[320]{0:T(512)} %refs_4_.1, s32[1]{0:T(128)S(6)} %copy.15.refs_5_, s32[1,240]{1,0:T(1,128)} %bitcast.21, f32[320]{0:T(512)} %refs_7_.1, ...), custom_call_target="tpu_custom_call" | custom-call | tf_op jit(solution)/shard_map/newton/pallas_call | solution.py:544
  34.4 0.7 %slice_bitcast_fusion = (f32[240,2,32]{0,2,1:T(8,128)}, f32[240,2,32]{0,2,1:T(8,128)}) fusion(f32[2,2,32,240]{3,2,1,0:T(8,128)S(1)} %newton.1), kind=kLoop, calls=%fused_computation | loop fusion | bytes 245760 | tf_op jit(solution)/shard_map/transpose | solution.py:583

commit v6 on v5

--- a/solution.py
+++ b/solution.py
@@ -383,7 +383,7 @@
     facing_inverse = inverse_of(beyond, there_parts)
     facing = applied(facing_inverse, beyond[3 * scen :])
 
-    def inside_product(k, v):
+    def inside_product(k, v, cols=slice(0, wide)):
         ends = select_dot(v, gather_tab[k], 2)
         f0, f1, t0, t1 = ends[:scen, :span], ends[scen:, :span], ends[:scen, span:], ends[scen:, span:]
         h00, h01, h10, h11 = (blocks[k, e] for e in range(4))
@@ -394,7 +394,7 @@
             ],
             axis=0,
         )
-        return select_dot(terms, scatter_tab[k], 2)
+        return select_dot(terms, scatter_tab[k, :, cols], 2)
 
     s, u = [start], [applied(diag_inverse, start)]
     s.append(inside_product(OWN, u[0]) + coupled(border, facing))
@@ -410,6 +410,8 @@
 
     told(1)
     tell(2)
+
+    sums = [inner(u[k // 2], s[k - k // 2]) for k in range(3)]
 
     for copy in far:
         copy.wait_recv()
@@ -434,15 +436,19 @@
         s.append(inside + coupled(border, facing))
         back = split(coupled(border_back, u[-1]))
         for k in range(2):
-            near, outside = back[k], coupled(outer_border[k], y_in[k]) if j == 2 else jnp.zeros_like(back[k])
-            product = inside_product(k, side[k]) + (join(near, outside) if k else join(outside, near))
-            side[k] = applied(side_inverse[k], product)
+            if j == 2:
+                outside = coupled(outer_border[k], y_in[k])
+                product = inside_product(k, side[k]) + (join(back[k], outside) if k else join(outside, back[k]))
+                side[k] = applied(side_inverse[k], product)
+            else:
+                cols = slice(0, LANES) if k else slice(LANES, wide)
+                product = inside_product(k, side[k], cols) + back[k]
+                side[k] = applied([f[:, cols] for f in side_inverse[k]], product)
         u.append(applied(diag_inverse, s[-1]))
         inside = inside_product(OWN, u[-1])
-    facing = join(split(side[0])[1], split(side[1])[0])
-    s.append(inside + coupled(border, facing))
-
-    def all_sum(tile):
+    s.append(inside + coupled(border, join(*side)))
+
+    def all_sum(tile, meanwhile):
         red_a[pl.ds(member, 1)] = tile[None]
         copies = []
         for d, peer in enumerate(peers_a):
@@ -456,6 +462,7 @@
             )
             copy.start()
             copies.append(copy)
+        ahead = meanwhile()
         for copy in copies:
             copy.wait_recv()
         pending.extend(copies)
@@ -481,11 +488,14 @@
         total = red_b[0]
         for k in range(1, outer):
             total = total + red_b[k]
-        return total
+        return total, ahead
 
     told(2)
-    parts = [inner(u[k // 2], s[k - k // 2]) for k in range(2 * ITERS)]
-    total = all_sum(jnp.concatenate([pack(parts[:4]), pack(parts[4:])], axis=0))
+    sums += [inner(u[k // 2], s[k - k // 2]) for k in range(3, 2 * ITERS)]
+    def bus_order():
+        return [select_dot(v, to_bus, 3) for v in u], [select_dot(v, to_bus, 3) for v in s]
+
+    total, (u, s) = all_sum(jnp.concatenate([pack(sums[:4]), pack(sums[4:])], axis=0), bus_order)
     moments = [total[k // 4 : k // 4 + 1] for k in range(2 * ITERS)]
     moments = [pltpu.roll(m, LANES - 32 * (k % 4), 1) if k % 4 else m for k, m in enumerate(moments)]
     gram = {(i, j): moments[i + j] + moments[i + j + 1] for i in range(ITERS) for j in range(i, ITERS)}
@@ -493,10 +503,9 @@
     w = [jnp.concatenate([jnp.concatenate([c, c], axis=1)] * 2, axis=0) for c in w]
     step = (1.0 + w[0]) * u[0] + (w[1] - 1.0) * u[1] + (1.0 + w[2]) * u[2] + (w[3] - 1.0) * u[3]
     residual = (1.0 - w[3]) * s[4] - (w[2] + w[3]) * s[3] - (w[1] + w[2]) * s[2] - (w[0] + w[1]) * s[1] - w[0] * s[0]
-    out = select_dot(jnp.concatenate([step, residual], axis=0), to_bus, 3)
     for c in range(2):
-        x_ref[c] = out[c * scen : (c + 1) * scen, :buses]
-        r_ref[c] = out[(2 + c) * scen : (3 + c) * scen, :buses]
+        x_ref[c] = step[c * scen : (c + 1) * scen, :buses]
+        r_ref[c] = residual[c * scen : (c + 1) * scen, :buses]
 
     for copy in pending:
         copy.wait_send()

time: 35.2 us -> 35.2 us (level)
  no operation moved by 1% of the time
where the time goes in v6:
time: 35.2 us; the launch traced here: 35 us
  Pallas kernels  33 us (94%)
  between operations  1.29 us (4%)
  local copies, waits for them, and re-layouts  0.66 us (2%)
    pallas_call x1, Pallas kernels, body(): pl.pallas_call(functools.partial(kernel, n, group), out_shape=pltpu.VMEM(...  33 us

profile of v6, /device:TPU:1, one launch (start us, length us, event | category | flops | bytes accessed | tf_op | source)
XLA Modules:
  0.0 35.0 jit_solution(1867366764844201986)
XLA Ops:
  1.3 33.0 %newton.1 = f32[2,2,32,240]{3,2,1,0:T(8,128)S(1)} custom-call(f32[32,240]{1,0:T(8,128)} %bitcast.19, f32[32,240]{1,0:T(8,128)} %bitcast.20, f32[2,32,240]{2,1,0:T(8,128)} %bitcast.18, s32[320]{0:T(512)} %refs_3_.1, s32[320]{0:T(512)} %refs_4_.1, s32[1]{0:T(128)S(6)} %copy.15.refs_5_, s32[1,240]{1,0:T(1,128)} %bitcast.21, f32[320]{0:T(512)} %refs_7_.1, ...), custom_call_target="tpu_custom_call" | custom-call | tf_op jit(solution)/shard_map/newton/pallas_call | solution.py:553
  34.3 0.7 %slice_bitcast_fusion = (f32[240,2,32]{0,2,1:T(8,128)}, f32[240,2,32]{0,2,1:T(8,128)}) fusion(f32[2,2,32,240]{3,2,1,0:T(8,128)S(1)} %newton.1), kind=kLoop, calls=%fused_computation | loop fusion | bytes 245760 | tf_op jit(solution)/shard_map/transpose | solution.py:592

commit v7 on v6

--- a/solution.py
+++ b/solution.py
@@ -208,6 +208,7 @@
 
     core = lax.rem(me, 2)
     mate = me + 1 - 2 * core
+    across = lax.rem(me + n - 1 + 2 * core, n)
     beyond_mate = lax.rem(me + n + 2 - 4 * core, n)
     pending = []
 
@@ -295,7 +296,10 @@
         a_out[half] = part
 
     pl.semaphore_wait(barrier, len(partners(n)))
-    a_near = [send(0, a_out.at[0], a_in.at[1, 0], prev), send(1, a_out.at[1], a_in.at[0, 1], nxt)]
+    a_near = [
+        send(0, a_out.at[core], a_in.at[1 - core, core], across),
+        send(1, a_out.at[1 - core], a_in.at[core, 1 - core], mate),
+    ]
 
     def local_blocks(k, volts, weight_p, weight_q, conduct, suscept):
         ends = select_dot(volts, gather_tab[k], 3)
@@ -325,7 +329,10 @@
     )
     for half, part in enumerate(split(own)):
         b_out[half] = part
-    b_near = [send(2, b_out.at[0], b_in.at[1, 0], prev), send(3, b_out.at[1], b_in.at[0, 1], nxt)]
+    b_near = [
+        send(2, b_out.at[core], b_in.at[1 - core, core], across),
+        send(3, b_out.at[1 - core], b_in.at[core, 1 - core], mate),
+    ]
 
     tell(0)
 
@@ -368,10 +375,10 @@
         v0, v1 = v[:scen], v[scen:]
         return jnp.concatenate([c[0] * v0 + c[1] * v1, c[2] * v0 + c[3] * v1], axis=0)
 
+    told(0)
+    tell(1)
     for copy in a_near:
         copy.wait_recv()
-    told(0)
-    tell(1)
     far.append(send(9, a_in.at[core, 1 - core], f_in.at[core], mate))
     here_parts, there_parts, border = coupling(payload, join(a_in[0, 1], a_in[1, 0]))
     border_back = (border[0], border[2], border[1], border[3])
@@ -402,10 +409,10 @@
     for half, part in enumerate(split(u[1])):
         x_out[half] = part
     vectors = [
-        send(12, x_out, x_in.at[1], prev),
-        send(13, x_out, x_in.at[0], nxt),
+        send(12, x_out, x_in.at[1 - core], across),
         send(14, x_out.at[0], y_in.at[1], prev2),
         send(15, x_out.at[1], y_in.at[0], nxt2),
+        send(13, x_out, x_in.at[core], mate),
     ]
 
     told(1)

time: 35.2 us -> 34.8 us (0.989)
  no operation moved by 1% of the time
where the time goes in v7:
time: 34.8 us; the launch traced here: 34.6 us
  Pallas kernels  32.7 us (94%)
  between operations  1.29 us (4%)
  local copies, waits for them, and re-layouts  0.66 us (2%)
    pallas_call x1, Pallas kernels, body(): pl.pallas_call(functools.partial(kernel, n, group), out_shape=pltpu.VMEM(...  32.7 us

profile of v7, /device:TPU:1, one launch (start us, length us, event | category | flops | bytes accessed | tf_op | source)
XLA Modules:
  0.0 34.6 jit_solution(6089691130376773642)
XLA Ops:
  1.3 32.7 %newton.1 = f32[2,2,32,240]{3,2,1,0:T(8,128)S(1)} custom-call(f32[32,240]{1,0:T(8,128)} %bitcast.19, f32[32,240]{1,0:T(8,128)} %bitcast.20, f32[2,32,240]{2,1,0:T(8,128)} %bitcast.18, s32[320]{0:T(512)} %refs_3_.1, s32[320]{0:T(512)} %refs_4_.1, s32[1]{0:T(128)S(6)} %copy.15.refs_5_, s32[1,240]{1,0:T(1,128)} %bitcast.21, f32[320]{0:T(512)} %refs_7_.1, ...), custom_call_target="tpu_custom_call" | custom-call | tf_op jit(solution)/shard_map/newton/pallas_call | solution.py:560
  34.0 0.7 %slice_bitcast_fusion = (f32[240,2,32]{0,2,1:T(8,128)}, f32[240,2,32]{0,2,1:T(8,128)}) fusion(f32[2,2,32,240]{3,2,1,0:T(8,128)S(1)} %newton.1), kind=kLoop, calls=%fused_computation | loop fusion | bytes 245760 | tf_op jit(solution)/shard_map/transpose | solution.py:599

commit v8 on v7

--- a/solution.py
+++ b/solution.py
@@ -300,6 +300,7 @@
         send(0, a_out.at[core], a_in.at[1 - core, core], across),
         send(1, a_out.at[1 - core], a_in.at[core, 1 - core], mate),
     ]
+    tell(0)
 
     def local_blocks(k, volts, weight_p, weight_q, conduct, suscept):
         ends = select_dot(volts, gather_tab[k], 3)
@@ -334,19 +335,17 @@
         send(3, b_out.at[1 - core], b_in.at[core, 1 - core], mate),
     ]
 
-    tell(0)
-
     w_out[0:scen] = weight_p
     w_out[scen : 2 * scen] = weight_q
     irow[5:7] = frow[0:2]
     w_out[2 * scen :] = irow[...]
     rows = pl.ds(0, 3 * scen)
     far = [
+        send(8, a_out.at[1 - core], f_in.at[core], beyond_mate),
         send(4, w_out, w_in.at[1], prev),
         send(5, w_out, w_in.at[0], nxt),
         send(6, a_out.at[1], a_in.at[1, 1], prev),
         send(7, a_out.at[0], a_in.at[0, 0], nxt),
-        send(8, a_out.at[1 - core], f_in.at[core], beyond_mate),
         send(10, b_out.at[1, rows], b_in.at[1, 1, rows], prev),
         send(11, b_out.at[0, rows], b_in.at[0, 0, rows], nxt),
     ]

time: 34.8 us -> 34.8 us (level)
  no operation moved by 1% of the time
where the time goes in v8:
time: 34.8 us; the launch traced here: 34.6 us
  Pallas kernels  32.7 us (94%)
  between operations  1.29 us (4%)
  local copies, waits for them, and re-layouts  0.66 us (2%)
    pallas_call x1, Pallas kernels, body(): pl.pallas_call(functools.partial(kernel, n, group), out_shape=pltpu.VMEM(...  32.7 us

profile of v8, /device:TPU:1, one launch (start us, length us, event | category | flops | bytes accessed | tf_op | source)
XLA Modules:
  0.0 34.6 jit_solution(14768302970902724490)
XLA Ops:
  1.3 32.7 %newton.1 = f32[2,2,32,240]{3,2,1,0:T(8,128)S(1)} custom-call(f32[32,240]{1,0:T(8,128)} %bitcast.19, f32[32,240]{1,0:T(8,128)} %bitcast.20, f32[2,32,240]{2,1,0:T(8,128)} %bitcast.18, s32[320]{0:T(512)} %refs_3_.1, s32[320]{0:T(512)} %refs_4_.1, s32[1]{0:T(128)S(6)} %copy.15.refs_5_, s32[1,240]{1,0:T(1,128)} %bitcast.21, f32[320]{0:T(512)} %refs_7_.1, ...), custom_call_target="tpu_custom_call" | custom-call | tf_op jit(solution)/shard_map/newton/pallas_call | solution.py:559
  34.0 0.7 %slice_bitcast_fusion = (f32[240,2,32]{0,2,1:T(8,128)}, f32[240,2,32]{0,2,1:T(8,128)}) fusion(f32[2,2,32,240]{3,2,1,0:T(8,128)S(1)} %newton.1), kind=kLoop, calls=%fused_computation | loop fusion | bytes 245760 | tf_op jit(solution)/shard_map/transpose | solution.py:598
